TPU v7x, 512 devices: a whole 4x8x8 slice. The times are simulated.
512 devices in a mesh: seq: 32 (over x, y), chan: 16 (over z, core).
Axes of the slice: x: 4, y: 8, z: 8, core: 2. Of those that a mesh axis runs over, the one named last changes fastest.
Arguments:
- tokens: bfloat16 [1536, 16384], P('chan', 'seq'), may hold values from -6 to 6
- gate_weight: bfloat16 [1536, 1536], P('chan'), may hold values from -0.15625 to 0.15625
- value_weight: bfloat16 [1536, 1536], P('chan'), may hold values from -0.15625 to 0.15625
- first_factor: bfloat16 [64, 256, 256], P('seq'), may hold values from -0.375 to 0.375
- second_factor: bfloat16 [256, 64, 64], P('seq'), may hold values from -0.75 to 0.75
- down_latent: bfloat16 [1536, 128], P('chan'), may hold values from -0.15625 to 0.15625
- up_latent: bfloat16 [1536, 128], P('chan'), may hold values from -0.5 to 0.5
- doc_lengths: int32 [64], replicated, may hold values from 1 to 8704, 16384 in all
- cotangent: bfloat16 [1536, 16384], P('chan', 'seq'), may hold values from -6 to 6
Outputs:
- hidden: bfloat16 [1536, 16384], P('chan', 'seq')
- d_gate_weight: float32 [1536, 1536], P('chan')
- d_value_weight: float32 [1536, 1536], P('chan')
- d_first: float32 [64, 256, 256], P('seq', 'chan')
- d_second: float32 [256, 64, 64], P('seq', 'chan')
- d_down: float32 [1536, 128], P('chan')
- d_up: float32 [1536, 128], P('chan')
Inputs may be any that keep to these rules, and one draw needn't show every extreme that they name: `doc_lengths`: the documents' lengths sum to 16384; the longest is exactly 8704 tokens.
All inputs are finite; a program needn't handle non-finite values.
Results may differ from a plain program's by a relative error of at most 0.0058.
Values may be sent and summed in bfloat16 or wider, within the bound.
No kernel may reach another device: no remote copies, remote signals or barrier semaphores. Data moves between devices by JAX's collectives and lax.ppermute only.
A program may use at most 64 MiB of HBM per device.

v0:
```python
import jax
import jax.numpy as jnp
from jax import lax
from jax.sharding import PartitionSpec as P


def body(
    tokens,
    gate_weight,
    value_weight,
    first_factor,
    second_factor,
    down_latent,
    up_latent,
    doc_lengths,
    cotangent,
):
    highest = lax.Precision.HIGHEST
    chan_rows, tok_cols = tokens.shape
    block_width = first_factor.shape[1]
    blocks_here = tok_cols // block_width
    gathered = lax.all_gather(tokens, "chan", axis=0, tiled=True)
    gate_pre = jnp.dot(gate_weight, gathered, preferred_element_type=jnp.float32)
    value_acc = jnp.dot(value_weight, gathered, preferred_element_type=jnp.float32)
    value_bf = value_acc.astype(jnp.bfloat16)
    doc_ends = jnp.cumsum(doc_lengths)
    doc_begins = doc_ends - doc_lengths
    position = lax.axis_index("seq") * tok_cols + jnp.arange(tok_cols, dtype=jnp.int32)
    member = (
        (position[None, :] >= doc_begins[:, None]) & (position[None, :] < doc_ends[:, None])
    ).astype(jnp.float32)
    len_scale = lax.rsqrt(doc_lengths.astype(jnp.float32))
    latent_part = jnp.einsum("ct,cl->lt", tokens, down_latent, preferred_element_type=jnp.float32)
    latent_full = lax.psum(latent_part, "chan")
    doc_sums = lax.psum(jnp.einsum("dt,lt->dl", member, latent_full, precision=highest), "seq")
    pooled = doc_sums * len_scale[:, None]
    up_float = up_latent.astype(jnp.float32)
    spread_rows = jnp.einsum("cl,dl->cd", up_float, pooled, precision=highest)
    summary = jnp.dot(spread_rows, member, precision=highest)
    blocked = value_bf.reshape(chan_rows, blocks_here, block_width)
    inner_mix = jnp.einsum(
        "ikj,cij->kic", first_factor, blocked, preferred_element_type=jnp.float32
    ).astype(jnp.bfloat16)
    columns = lax.all_to_all(inner_mix, "seq", split_axis=0, concat_axis=1, tiled=True)
    outer_mix = jnp.einsum(
        "kmi,kic->kmc", second_factor, columns, preferred_element_type=jnp.float32
    ).astype(jnp.bfloat16)
    mixed_back = lax.all_to_all(outer_mix, "seq", split_axis=1, concat_axis=0, tiled=True)
    mixed = (
        jnp.transpose(mixed_back, (2, 1, 0)).reshape(chan_rows, tok_cols).astype(jnp.float32)
        + summary
    )
    sig = jax.nn.sigmoid(gate_pre)
    act = gate_pre * sig
    hidden = (act * mixed).astype(jnp.bfloat16)
    upstream = cotangent.astype(jnp.float32)
    d_mixed = upstream * act
    d_mixed_bf = d_mixed.astype(jnp.bfloat16)
    d_gate_bf = (upstream * mixed * sig * (1.0 + gate_pre * (1.0 - sig))).astype(jnp.bfloat16)
    d_send = jnp.transpose(d_mixed_bf.reshape(chan_rows, blocks_here, block_width), (2, 1, 0))
    d_outer = lax.all_to_all(d_send, "seq", split_axis=0, concat_axis=1, tiled=True)
    d_inner = jnp.einsum(
        "kmi,kmc->kic", second_factor, d_outer, preferred_element_type=jnp.float32
    ).astype(jnp.bfloat16)
    d_second_part = jnp.einsum("kmc,kic->kmi", d_outer, columns, preferred_element_type=jnp.float32)
    d_rows = lax.all_to_all(d_inner, "seq", split_axis=1, concat_axis=0, tiled=True)
    d_value_bf = (
        jnp.einsum("ikj,kic->cij", first_factor, d_rows, preferred_element_type=jnp.float32)
        .astype(jnp.bfloat16)
        .reshape(chan_rows, tok_cols)
    )
    d_first_part = jnp.einsum("kic,cij->ikj", d_rows, blocked, preferred_element_type=jnp.float32)
    per_doc = jnp.einsum("ct,dt->cd", d_mixed, member, precision=highest)
    d_up_part = jnp.einsum("cd,dl->cl", per_doc, pooled, precision=highest)
    d_pooled = lax.psum(
        jnp.einsum("cd,cl->dl", per_doc, up_float, precision=highest), ("seq", "chan")
    )
    d_latent_bf = jnp.einsum(
        "dl,dt->lt", d_pooled * len_scale[:, None], member, precision=highest
    ).astype(jnp.bfloat16)
    d_down_part = jnp.einsum("ct,lt->cl", tokens, d_latent_bf, preferred_element_type=jnp.float32)
    both_grads = jnp.concatenate([d_gate_bf, d_value_bf], axis=0)
    d_proj = jnp.einsum("ot,it->oi", both_grads, gathered, preferred_element_type=jnp.float32)
    d_proj, d_down, d_up = lax.psum((d_proj, d_down_part, d_up_part), "seq")
    d_first, d_second = (
        lax.psum_scatter(d_first_part, "chan", scatter_dimension=1, tiled=True),
        lax.psum_scatter(d_second_part, "chan", scatter_dimension=1, tiled=True),
    )
    return (hidden, d_proj[:chan_rows], d_proj[chan_rows:], d_first, d_second, d_down, d_up)


def solution(mesh):
    in_specs = (
        P("chan", "seq"),
        P("chan", None),
        P("chan", None),
        P("seq", None, None),
        P("seq", None, None),
        P("chan", None),
        P("chan", None),
        P(),
        P("chan", "seq"),
    )
    out_specs = (
        P("chan", "seq"),
        P("chan", None),
        P("chan", None),
        P("seq", "chan", None),
        P("seq", "chan", None),
        P("chan", None),
        P("chan", None),
    )
    return jax.shard_map(body, mesh=mesh, in_specs=in_specs, out_specs=out_specs, check_vma=False)
```

profile of v0, /device:TPU:1, one launch (start us, length us, event | category | flops | bytes accessed | tf_op | source)
XLA Modules:
  0.0 782.3 jit_solution(4157676948622246798)
XLA Ops:
  7.2 1.9 fusion.36
  9.2 0.7 all-gather.2.cloned.1.call-update
  9.9 0.7 copy.46
  10.7 0.1 reduce
  10.8 0.7 sub.6
  11.5 0.7 convert_rsqrt_fusion
  12.2 120.5 %all-reduce.5.cloned.1.call-done = f32[128,512]{1,0:T(8,128)} async-done(((f32[128,512]{1,0:T(8,128)}), f32[128,512]{1,0:T(8,128)}) %all-reduce.5.cloned.1.call-update) | async-done | bytes 262160 | tf_op jit(solution)/shard_map/psum | solution.py:34
  132.6 1.2 fusion.32
  133.9 115.1 %psum.43 = f32[64,128]{1,0:T(8,128)S(1)} all-reduce(f32[64,128]{1,0:T(8,128)S(1)} %fusion.32), channel_id=1, replica_groups=mesh['seq'=32,'chan'=16] {'seq'}, use_global_device_ids=true, to_apply=%region_2.3 | all-reduce | flops 8192 | bytes 65536 | tf_op jit(solution)/shard_map/psum | solution.py:35
  249.0 1.8 convolution_convert_fusion.4
  250.9 0.2 fusion.2
  251.1 0.8 copy.40
  251.9 3.9 all-to-all-start
  255.8 0.2 fusion.26
  256.0 8.9 %all-to-all-done = bf16[256,2,96]{2,1,0:T(2,128)(2,1)S(1)} async-done(((bf16[256,2,96]{2,1,0:T(2,128)(2,1)}), bf16[256,2,96]{2,1,0:T(2,128)(2,1)S(1)}, u32[]{:S(2)}, u32[]{:S(2)}) %all-to-all-start) | async-done | bytes 98336 | tf_op jit(solution)/shard_map/all_to_all | solution.py:44
  264.9 0.1 copy.42
  265.1 0.2 fusion.1
  265.2 0.7 copy.43
  266.0 4.0 all-to-all-start.1
  270.0 0.4 fusion.35
  270.4 8.7 %all-to-all-done.1 = bf16[8,64,96]{2,0,1:T(8,128)(2,1)S(1)} async-done(((bf16[8,64,96]{2,0,1:T(8,128)(2,1)}), bf16[8,64,96]{2,0,1:T(8,128)(2,1)S(1)}, u32[]{:S(2)}, u32[]{:S(2)}) %all-to-all-start.1) | async-done | bytes 98336 | tf_op jit(solution)/shard_map/all_to_all | solution.py:48
  279.1 0.1 copy.62
  279.3 1.0 fusion.6
  280.3 0.1 copy.47
  280.5 12.6 %all_to_all.66 = bf16[256,2,96]{2,1,0:T(2,128)(2,1)S(1)} all-to-all(bf16[256,2,96]{2,1,0:T(2,128)(2,1)S(1)} %bitcast.82), channel_id=1, replica_groups=mesh['seq'=32,'chan'=16] {'seq'}, dimensions={0} | all-to-all | bytes 196608 | tf_op jit(solution)/shard_map/all_to_all | solution.py:61
  293.1 0.1 copy.49
  293.2 0.2 fusion
  293.4 0.7 copy.51
  294.2 4.6 all-to-all-start.3
  298.8 0.2 fusion.37
  299.0 0.9 copy.57
  300.0 8.0 %all-to-all-done.3 = bf16[8,64,96]{2,0,1:T(8,128)(2,1)S(1)} async-done(((bf16[8,64,96]{2,0,1:T(8,128)(2,1)}), bf16[8,64,96]{2,0,1:T(8,128)(2,1)S(1)}, u32[]{:S(2)}, u32[]{:S(2)}) %all-to-all-start.3) | async-done | bytes 98336 | tf_op jit(solution)/shard_map/all_to_all | solution.py:66
  307.9 0.2 fusion.3
  308.2 1.7 fusion.7
  310.0 0.3 fusion.12
  310.3 0.1 fusion.38
  310.4 126.9 %psum.45 = f32[64,128]{1,0:T(8,128)S(1)} all-reduce(f32[64,128]{1,0:T(8,128)S(1)} %fusion.38), channel_id=1, replica_groups=mesh['seq'=32,'chan'=16] {'seq','chan'}, use_global_device_ids=true, to_apply=%region_6.7 | all-reduce | flops 8192 | bytes 65536 | tf_op jit(solution)/shard_map/psum | solution.py:75
  437.3 0.9 fusion.24
  438.3 0.4 convolution_convert_fusion.2
  438.6 0.8 convolution_bitcast_fusion
  439.5 1.0 fusion.14
  440.6 1.3 copy.58
  441.9 110.7 %all-reduce.7.cloned.1.call-done = f32[192,1536]{1,0:T(8,128)} async-done(((f32[192,1536]{1,0:T(8,128)}), f32[192,1536]{1,0:T(8,128)}) %all-reduce.7.cloned.1.call-update) | async-done | bytes 1179664 | tf_op jit(solution)/shard_map/psum | solution.py:84
  552.6 2.3 fusion.34
  555.0 153.9 %all-reduce.9.cloned.1.call-done = (f32[96,128]{1,0:T(8,128)}, f32[96,128]{1,0:T(8,128)}) async-done(((f32[96,128]{1,0:T(8,128)}, f32[96,128]{1,0:T(8,128)}), (f32[96,128]{1,0:T(8,128)}, f32[96,128]{1,0:T(8,128)})) %all-reduce.9.cloned.1.call-update) | async-done | bytes 98320 | tf_op jit(solution)/shard_map/psum | solution.py:84
  708.9 63.7 %reduce-scatter.3.cloned.1.call-done = f32[2,16,256]{2,1,0:T(8,128)} async-done(((f32[2,256,256]{2,1,0:T(8,128)}), f32[2,16,256]{2,1,0:T(8,128)}) %reduce-scatter.3.cloned.1.call-update) | async-done | bytes 32784 | tf_op jit(solution)/shard_map/reduce_scatter | solution.py:86
  772.6 1.4 copy.89
  774.0 1.4 copy.90
  (36 shorter events, 0.6 us)
Async XLA Ops:
  7.2 241.9 %copy-start = (bf16[96,1536]{1,0:T(8,128)(2,1)S(1)}, bf16[96,1536]{1,0:T(8,128)(2,1)}, u32[]{:S(2)}) copy-start(bf16[96,1536]{1,0:T(8,128)(2,1)} %param.11) | copy-start | bytes 884740
  7.2 243.7 %copy-start.2 = (bf16[2,256,256]{2,1,0:T(8,128)(2,1)S(1)}, bf16[2,256,256]{2,1,0:T(8,128)(2,1)}, u32[]{:S(2)}) copy-start(bf16[2,256,256]{2,1,0:T(8,128)(2,1)} %param.12) | copy-start | bytes 786436
  7.2 125.4 %all-reduce.5.cloned.1.call-start = ((), (), s32[]{:S(2)}) async-start(), calls=%async_computation.7 | async-start | bytes 524288 | tf_op jit(solution)/shard_map/psum | solution.py:34
  9.1 239.9 %all-gather.2.cloned.1.call-start = ((), (), s32[]{:S(2)}) async-start(), calls=%async_computation.6 | async-start | bytes 1671168 | tf_op jit(solution)/shard_map/all_gather | solution.py:22
  12.2 243.6 %copy-start.6 = (bf16[96,128]{1,0:T(8,128)(2,1)S(1)}, bf16[96,128]{1,0:T(8,128)(2,1)}, u32[]{:S(2)}) copy-start(bf16[96,128]{1,0:T(8,128)(2,1)} %param.15) | copy-start | bytes 73732
  249.0 16.0 %copy-start.4 = (bf16[8,64,64]{2,1,0:T(8,128)(2,1)S(1)}, bf16[8,64,64]{2,1,0:T(8,128)(2,1)}, u32[]{:S(2)}) copy-start(bf16[8,64,64]{2,1,0:T(8,128)(2,1)} %param.13) | copy-start | bytes 196612
  250.9 19.1 %copy-start.1 = (bf16[1536,512]{1,0:T(8,128)(2,1)S(1)}, bf16[1536,512]{1,0:T(8,128)(2,1)}, u32[]{:S(2)}) copy-start(bf16[1536,512]{1,0:T(8,128)(2,1)} %all-gather.2.cloned.1.call-done) | copy-start | bytes 4718596
  250.9 19.1 %copy-start.5 = (bf16[96,1536]{1,0:T(8,128)(2,1)S(1)}, bf16[96,1536]{1,0:T(8,128)(2,1)}, u32[]{:S(2)}) copy-start(bf16[96,1536]{1,0:T(8,128)(2,1)} %param.10) | copy-start | bytes 884740
  251.9 13.0 %all-to-all-start = ((bf16[256,2,96]{2,1,0:T(2,128)(2,1)}), bf16[256,2,96]{2,1,0:T(2,128)(2,1)S(1)}, u32[]{:S(2)}, u32[]{:S(2)}) async-start(bf16[256,2,96]{2,1,0:T(2,128)(2,1)} %copy.40), calls=%async_computation | async-start | bytes 262144 | tf_op jit(solution)/shard_map/all_to_all | solution.py:44
  266.0 13.3 %copy-start.7 = (bf16[96,512]{1,0:T(8,128)(2,1)S(1)}, bf16[96,512]{1,0:T(8,128)(2,1)}, u32[]{:S(2)}) copy-start(bf16[96,512]{1,0:T(8,128)(2,1)} %param.17) | copy-start | bytes 294916
  266.0 13.1 %all-to-all-start.1 = ((bf16[8,64,96]{2,0,1:T(8,128)(2,1)}), bf16[8,64,96]{2,0,1:T(8,128)(2,1)S(1)}, u32[]{:S(2)}, u32[]{:S(2)}) async-start(bf16[8,64,96]{2,0,1:T(8,128)(2,1)} %copy.43), calls=%async_computation.1 | async-start | bytes 262144 | tf_op jit(solution)/shard_map/all_to_all | solution.py:48
  294.2 13.7 %all-to-all-start.3 = ((bf16[8,64,96]{2,0,1:T(8,128)(2,1)}), bf16[8,64,96]{2,0,1:T(8,128)(2,1)S(1)}, u32[]{:S(2)}, u32[]{:S(2)}) async-start(bf16[8,64,96]{2,0,1:T(8,128)(2,1)} %copy.51), calls=%async_computation.3 | async-start | bytes 262144 | tf_op jit(solution)/shard_map/all_to_all | solution.py:66
  298.8 141.8 %reduce-scatter.5.cloned.1.call-start = ((), (), s32[]{:S(2)}) async-start(), calls=%async_computation.10 | async-start | bytes 278528 | tf_op jit(solution)/shard_map/reduce_scatter | solution.py:87
  299.9 252.7 %all-reduce.7.cloned.1.call-start = ((), (), s32[]{:S(2)}) async-start(), calls=%async_computation.8 | async-start | bytes 2359296 | tf_op jit(solution)/shard_map/psum | solution.py:84
  309.9 128.8 %copy-start.3 = (bf16[96,512]{1,0:T(8,128)(2,1)S(1)}, bf16[96,512]{1,0:T(8,128)(2,1)}, u32[]{:S(2)}) copy-start(bf16[96,512]{1,0:T(8,128)(2,1)} %param.9) | copy-start | bytes 294916
  309.9 399.0 %all-reduce.9.cloned.1.call-start = ((), (), s32[]{:S(2)}) async-start(), calls=%async_computation.11 | async-start | bytes 196608 | tf_op jit(solution)/shard_map/psum | solution.py:84
  439.5 333.1 %reduce-scatter.3.cloned.1.call-start = ((), (), s32[]{:S(2)}) async-start(), calls=%async_computation.9 | async-start | bytes 557056 | tf_op jit(solution)/shard_map/reduce_scatter | solution.py:86
Sparse Core Ops, SparseCore 0:
  10.9 121.7 all-reduce.4
  134.8 42.5 all-gather.1
  302.9 89.1 reduce-scatter.4
  395.4 157.1 all-reduce.6
  556.5 152.3 all-reduce.8
  712.1 60.4 reduce-scatter.2
where the time goes:
time: 785 us; the launch traced here: 782 us
  waiting for transfers between devices  475 us (61%)
  blocking collectives  255 us (32%)
  between operations  14.4 us (2%)
  matrix products  12.8 us (2%)
  starting transfers between devices  12.7 us (2%)
  local copies, waits for them, and re-layouts  11 us (1%)
    psum x2, waiting for transfers between devices, body(): d_proj, d_down, d_up = lax.psum((d_proj, d_down_part, d_up_part), 'seq')  265 us
    psum x1, blocking collectives, body(): lax.psum(jnp.einsum('cd,cl->dl', per_doc, up_float, precision=highest), (...  127 us
    psum x1, waiting for transfers between devices, body(): latent_full = lax.psum(latent_part, 'chan')  120 us
    psum x1, blocking collectives, body(): lax.psum(jnp.einsum('dt,lt->dl', member, latent_full, precision=highest),...  115 us
    reduce_scatter x1, waiting for transfers between devices, body(): lax.psum_scatter(d_first_part, 'chan', scatter_dimension=1, tiled=True)  63.7 us
  transfers between devices with their start and end apart: 9, of which 7 were waited for; matrix products, arithmetic and copies ran while one was open for 2% of the time, Pallas kernels for 0%

commit v1 on v0

v1 whole, which is shorter than its diff:
```python
import jax
import jax.numpy as jnp
from jax import lax
from jax.sharding import PartitionSpec as P


HIGHEST = lax.Precision.HIGHEST


def seq_exchange(x):
    return lax.all_to_all(x, "seq", 0, 0, tiled=True)


def chan_exchange(x):
    return lax.all_to_all(x, "chan", 0, 0, tiled=True)


def body(
    tokens,
    gate_weight,
    value_weight,
    first_factor,
    second_factor,
    down_latent,
    up_latent,
    doc_lengths,
    cotangent,
):
    n_seq = lax.axis_size("seq")
    n_chan = lax.axis_size("chan")
    chan_rows, tok_cols = tokens.shape
    blocks_here, block_width, _ = first_factor.shape
    k_here, n_blk2, _ = second_factor.shape
    lat = down_latent.shape[1]
    n_doc = doc_lengths.shape[0]
    docs_here = n_doc // n_seq
    me = lax.axis_index("seq")

    packed = jnp.concatenate([tokens, down_latent], axis=1)
    gathered_all = lax.all_gather(packed, "chan", axis=0, tiled=True)
    gathered = gathered_all[:, :tok_cols]
    down_full = gathered_all[:, tok_cols:]

    doc_ends = jnp.cumsum(doc_lengths)
    doc_begins = doc_ends - doc_lengths
    position = me * tok_cols + jnp.arange(tok_cols, dtype=jnp.int32)
    member = (
        (position[None, :] >= doc_begins[:, None]) & (position[None, :] < doc_ends[:, None])
    ).astype(jnp.float32)
    len_scale = lax.rsqrt(doc_lengths.astype(jnp.float32))

    gate_pre = jnp.dot(gate_weight, gathered, preferred_element_type=jnp.float32)
    value_bf = jnp.dot(value_weight, gathered, preferred_element_type=jnp.float32).astype(
        jnp.bfloat16
    )
    latent = jnp.einsum("ct,cl->lt", gathered, down_full, preferred_element_type=jnp.float32)
    doc_lat_part = jnp.einsum("dt,lt->dl", member, latent, precision=HIGHEST)
    xdoc_part = jnp.einsum(
        "ct,dt->cd", tokens, member.astype(jnp.bfloat16), preferred_element_type=jnp.float32
    )

    blocked = value_bf.reshape(chan_rows, blocks_here, block_width)
    inner_mix = jnp.einsum(
        "ikj,cij->ikc", first_factor, blocked, preferred_element_type=jnp.float32
    ).astype(jnp.bfloat16)

    sig = jax.nn.sigmoid(gate_pre)
    act = gate_pre * sig
    upstream = cotangent.astype(jnp.float32)
    d_mixed = upstream * act
    d_mixed_bf = d_mixed.astype(jnp.bfloat16)
    per_doc_part = jnp.einsum("ct,dt->cd", d_mixed, member, precision=HIGHEST)

    inner_send = inner_mix.reshape(blocks_here, n_seq, k_here, chan_rows).transpose(1, 0, 2, 3)
    d_send = d_mixed_bf.reshape(chan_rows, blocks_here, n_seq, k_here).transpose(2, 1, 3, 0)
    recv2 = seq_exchange(jnp.concatenate([inner_send, d_send], axis=3))
    columns = recv2[..., :chan_rows].reshape(n_seq * blocks_here, k_here, chan_rows)
    d_outer = recv2[..., chan_rows:].reshape(n_seq * blocks_here, k_here, chan_rows)

    small_send = jnp.concatenate(
        [
            doc_lat_part.reshape(n_seq, docs_here * lat),
            per_doc_part.reshape(chan_rows, n_seq, docs_here)
            .transpose(1, 0, 2)
            .reshape(n_seq, chan_rows * docs_here),
            xdoc_part.reshape(chan_rows, n_seq, docs_here)
            .transpose(1, 0, 2)
            .reshape(n_seq, chan_rows * docs_here),
        ],
        axis=1,
    )
    small_red = jnp.sum(seq_exchange(small_send), axis=0)
    n_a = docs_here * lat
    n_b = chan_rows * docs_here
    scale_here = lax.dynamic_slice(len_scale, (me * docs_here,), (docs_here,))
    pooled_here = small_red[:n_a].reshape(docs_here, lat) * scale_here[:, None]
    per_doc_here = small_red[n_a : n_a + n_b].reshape(chan_rows, docs_here)
    xdoc_here = small_red[n_a + n_b :].reshape(chan_rows, docs_here)

    up_float = up_latent.astype(jnp.float32)
    g_part = jnp.einsum("cd,cl->dl", per_doc_here, up_float, precision=HIGHEST)
    g_here = jnp.sum(
        chan_exchange(jnp.broadcast_to(g_part.reshape(1, n_a), (n_chan, n_a))), axis=0
    )

    outer_mix = jnp.einsum(
        "kmi,ikc->mkc", second_factor, columns, preferred_element_type=jnp.float32
    ).astype(jnp.bfloat16)
    d_inner = jnp.einsum(
        "kmi,mkc->ikc", second_factor, d_outer, preferred_element_type=jnp.float32
    ).astype(jnp.bfloat16)
    d_second_part = jnp.einsum(
        "mkc,ikc->kmi", d_outer, columns, preferred_element_type=jnp.float32
    )

    outer_send = outer_mix.reshape(n_seq, blocks_here, k_here, chan_rows)
    dinner_send = d_inner.reshape(n_seq, blocks_here, k_here, chan_rows)
    recv3 = seq_exchange(jnp.concatenate([outer_send, dinner_send], axis=3))
    outer_tok = (
        recv3[..., :chan_rows].transpose(3, 1, 0, 2).reshape(chan_rows, tok_cols).astype(jnp.float32)
    )
    d_rows = recv3[..., chan_rows:].transpose(1, 0, 2, 3).reshape(
        blocks_here, n_seq * k_here, chan_rows
    )
    piece = jnp.concatenate(
        [pooled_here.reshape(n_a), per_doc_here.reshape(n_b), xdoc_here.reshape(n_b)]
    )
    gath3 = seq_exchange(jnp.broadcast_to(piece[None, :], (n_seq, piece.shape[0])))
    pooled = gath3[:, :n_a].reshape(n_doc, lat)
    per_doc = (
        gath3[:, n_a : n_a + n_b].reshape(n_seq, chan_rows, docs_here).transpose(1, 0, 2)
    ).reshape(chan_rows, n_doc)
    xdoc = (
        gath3[:, n_a + n_b :].reshape(n_seq, chan_rows, docs_here).transpose(1, 0, 2)
    ).reshape(chan_rows, n_doc)

    spread = jnp.einsum("dl,cl->cd", pooled, up_float, precision=HIGHEST)
    summary = jnp.dot(spread, member, precision=HIGHEST)
    mixed = outer_tok + summary
    hidden = (act * mixed).astype(jnp.bfloat16)
    d_gate_bf = (upstream * mixed * sig * (1.0 + gate_pre * (1.0 - sig))).astype(jnp.bfloat16)

    d_value_bf = (
        jnp.einsum("ikj,ikc->cij", first_factor, d_rows, preferred_element_type=jnp.float32)
        .astype(jnp.bfloat16)
        .reshape(chan_rows, tok_cols)
    )
    d_first_part = jnp.einsum("ikc,cij->ikj", d_rows, blocked, preferred_element_type=jnp.float32)
    d_up = jnp.einsum("cd,dl->cl", per_doc, pooled, precision=HIGHEST)

    both_grads = jnp.concatenate([d_gate_bf, d_value_bf], axis=0)
    d_proj_part = jnp.einsum("ot,it->oi", both_grads, gathered, preferred_element_type=jnp.float32)
    rows_here = 2 * chan_rows // n_seq
    width = d_proj_part.shape[1]

    proj_red = jnp.sum(seq_exchange(d_proj_part.reshape(n_seq, rows_here, width)), axis=0)
    k_part = block_width // n_chan
    m_part = n_blk2 // n_chan
    first_send = (
        d_first_part.reshape(blocks_here, n_chan, k_part, block_width)
        .transpose(1, 0, 2, 3)
        .reshape(n_chan, -1)
    )
    second_send = (
        d_second_part.reshape(k_here, n_chan, m_part, n_blk2).transpose(1, 0, 2, 3).reshape(n_chan, -1)
    )
    fac_red = jnp.sum(chan_exchange(jnp.concatenate([first_send, second_send], axis=1)), axis=0)
    n_f = blocks_here * k_part * block_width
    d_first = fac_red[:n_f].reshape(blocks_here, k_part, block_width)
    d_second = fac_red[n_f:].reshape(k_here, m_part, n_blk2)

    piece5 = jnp.concatenate([proj_red.reshape(-1), g_here])
    gath5 = seq_exchange(jnp.broadcast_to(piece5[None, :], (n_seq, piece5.shape[0])))
    n_p = rows_here * width
    d_proj = gath5[:, :n_p].reshape(2 * chan_rows, width)
    d_pooled = gath5[:, n_p:].reshape(n_doc, lat) * len_scale[:, None]
    d_down = jnp.einsum(
        "cd,dl->cl", xdoc, d_pooled.astype(jnp.bfloat16).astype(jnp.float32), precision=HIGHEST
    )
    return (hidden, d_proj[:chan_rows], d_proj[chan_rows:], d_first, d_second, d_down, d_up)


def solution(mesh):
    in_specs = (
        P("chan", "seq"),
        P("chan", None),
        P("chan", None),
        P("seq", None, None),
        P("seq", None, None),
        P("chan", None),
        P("chan", None),
        P(),
        P("chan", "seq"),
    )
    out_specs = (
        P("chan", "seq"),
        P("chan", None),
        P("chan", None),
        P("seq", "chan", None),
        P("seq", "chan", None),
        P("chan", None),
        P("chan", None),
    )
    return jax.shard_map(body, mesh=mesh, in_specs=in_specs, out_specs=out_specs, check_vma=False)
```

time: 785 us -> 259 us (0.33)
  waiting for transfers between devices: 475 us -> 162 us
  blocking collectives: 255 us -> 0 us
  starting transfers between devices: 12.7 us -> 49 us
    psum x3 -> x0, waiting for transfers between devices: 385 us -> none  [the longest x2 265 us: body(): d_proj, d_down, d_up = lax.psum((d_proj, d_down_part, d_up_part), 'seq')]
    psum x2 -> x0, blocking collectives: 242 us -> none  [the longest x1 127 us: body(): lax.psum(jnp.einsum('cd,cl->dl', per_doc, up_float, precision=highest), (...]
    all_to_all x3 -> x8, waiting for transfers between devices: 25.6 us -> 114 us  [the longest x6 92.6 us: seq_exchange(): return lax.all_to_all(x, 'seq', 0, 0, tiled=True)]
    reduce_scatter x2 -> x0, waiting for transfers between devices: 63.7 us -> none  [the longest x1 63.7 us: body(): lax.psum_scatter(d_first_part, 'chan', scatter_dimension=1, tiled=True)]
    all_gather x1, waiting for transfers between devices: 0.01 us -> 47.7 us  [body(): gathered_all = lax.all_gather(packed, 'chan', axis=0, tiled=True)]
    all_to_all x3 -> x8, starting transfers between devices: 12.4 us -> 49 us  [the longest x6 32.8 us: seq_exchange(): return lax.all_to_all(x, 'seq', 0, 0, tiled=True)]
    all_to_all x1 -> x0, blocking collectives: 12.6 us -> none  [body(): lax.all_to_all(d_send, 'seq', split_axis=0, concat_axis=1, tiled=True)]
  transfers between devices with their start and end apart: 9 -> 9, of which waited for: 7 -> 9; matrix products, arithmetic and copies ran while one was open for 2% -> 7% of each run, Pallas kernels for 0% -> 0%
where the time goes in v1:
time: 259 us; the launch traced here: 258 us
  waiting for transfers between devices  162 us (63%)
  starting transfers between devices  49 us (19%)
  local copies, waits for them, and re-layouts  15.8 us (6%)
  between operations  14.6 us (6%)
  matrix products  11.5 us (4%)
  other arithmetic  5.15 us (2%)
    all_to_all x6, waiting for transfers between devices, seq_exchange(): return lax.all_to_all(x, 'seq', 0, 0, tiled=True)  92.6 us
    all_gather x1, waiting for transfers between devices, body(): gathered_all = lax.all_gather(packed, 'chan', axis=0, tiled=True)  47.7 us
    all_to_all x6, starting transfers between devices, seq_exchange(): return lax.all_to_all(x, 'seq', 0, 0, tiled=True)  32.8 us
    all_to_all x2, waiting for transfers between devices, chan_exchange(): return lax.all_to_all(x, 'chan', 0, 0, tiled=True)  21.9 us
    all_to_all x2, starting transfers between devices, chan_exchange(): return lax.all_to_all(x, 'chan', 0, 0, tiled=True)  16.2 us
  transfers between devices with their start and end apart: 9, of which 9 were waited for; matrix products, arithmetic and copies ran while one was open for 7% of the time, Pallas kernels for 0%

profile of v1, /device:TPU:1, one launch (start us, length us, event | category | flops | bytes accessed | tf_op | source)
XLA Modules:
  0.0 258.2 jit_solution(9266337359368972084)
XLA Ops:
  7.2 1.6 pad_maximum_fusion.2
  8.9 0.7 copy.140
  9.8 0.7 sub.6
  10.5 1.1 fusion.27
  11.8 47.7 %all-gather.2.cloned.1.call-done = bf16[1536,640]{1,0:T(8,128)(2,1)} async-done(((bf16[96,640]{1,0:T(8,128)(2,1)}), bf16[1536,640]{1,0:T(8,128)(2,1)}) %all-gather.2.cloned.1.call-update) | async-done | bytes 1966096 | tf_op jit(solution)/shard_map/all_gather | solution.py:40
  59.4 2.1 fusion.4
  61.5 0.3 fusion.31
  61.8 0.4 fusion.17
  62.3 0.3 fusion.16
  63.1 0.7 all_to_all.39
  63.8 9.3 %all-to-all-start.2 = ((f32[32,1,640]{2,1,0:T(1,128)}), f32[32,1,640]{2,1,0:T(1,128)S(1)}, u32[]{:S(2)}, u32[]{:S(2)}) async-start(f32[32,1,640]{2,1,0:T(1,128)} %all_to_all.39), calls=%async_computation.2 | async-start | bytes 163840 | tf_op jit(solution)/shard_map/all_to_all | solution.py:11
  73.1 1.3 convolution_convert_fusion.2
  74.8 0.3 copy-done.10
  75.3 0.7 copy.133
  76.0 6.0 %all-to-all-done.2 = f32[32,1,640]{2,1,0:T(1,128)S(1)} async-done(((f32[32,1,640]{2,1,0:T(1,128)}), f32[32,1,640]{2,1,0:T(1,128)S(1)}, u32[]{:S(2)}, u32[]{:S(2)}) %all-to-all-start.2) | async-done | bytes 81952 | tf_op jit(solution)/shard_map/all_to_all | solution.py:11
  82.0 3.9 %all-to-all-start = ((bf16[32,2,8,192]{3,2,1,0:T(8,128)(2,1)}), bf16[32,2,8,192]{3,2,1,0:T(8,128)(2,1)S(1)}, u32[]{:S(2)}, u32[]{:S(2)}) async-start(bf16[32,2,8,192]{3,2,1,0:T(8,128)(2,1)} %copy.133), calls=%async_computation | async-start | bytes 524288 | tf_op jit(solution)/shard_map/all_to_all | solution.py:11
  86.0 0.4 copy-done.14
  86.6 9.0 %all-to-all-done = bf16[32,2,8,192]{3,2,1,0:T(8,128)(2,1)S(1)} async-done(((bf16[32,2,8,192]{3,2,1,0:T(8,128)(2,1)}), bf16[32,2,8,192]{3,2,1,0:T(8,128)(2,1)S(1)}, u32[]{:S(2)}, u32[]{:S(2)}) %all-to-all-start) | async-done | bytes 196640 | tf_op jit(solution)/shard_map/all_to_all | solution.py:11
  95.5 0.7 broadcast_in_dim.8
  96.2 6.2 %all-to-all-start.3 = ((f32[32,1,640]{2,1,0:T(1,128)}), f32[32,1,640]{2,1,0:T(1,128)S(1)}, u32[]{:S(2)}, u32[]{:S(2)}) async-start(f32[32,1,640]{2,1,0:T(1,128)} %broadcast_in_dim.8), calls=%async_computation.3 | async-start | bytes 163840 | tf_op jit(solution)/shard_map/all_to_all | solution.py:11
  102.8 0.5 copy-done.2
  104.1 0.8 pad_maximum_fusion.1
  105.0 6.4 %all-to-all-done.3 = f32[32,1,640]{2,1,0:T(1,128)S(1)} async-done(((f32[32,1,640]{2,1,0:T(1,128)}), f32[32,1,640]{2,1,0:T(1,128)S(1)}, u32[]{:S(2)}, u32[]{:S(2)}) %all-to-all-start.3) | async-done | bytes 81952 | tf_op jit(solution)/shard_map/all_to_all | solution.py:11
  111.4 3.9 %all-to-all-start.1 = ((bf16[32,2,8,192]{3,2,1,0:T(8,128)(2,1)}), bf16[32,2,8,192]{3,2,1,0:T(8,128)(2,1)S(1)}, u32[]{:S(2)}, u32[]{:S(2)}) async-start(bf16[32,2,8,192]{3,2,1,0:T(8,128)(2,1)} %pad_maximum_fusion.1), calls=%async_computation.1 | async-start | bytes 524288 | tf_op jit(solution)/shard_map/all_to_all | solution.py:11
  115.8 9.2 %all-to-all-done.1 = bf16[32,2,8,192]{3,2,1,0:T(8,128)(2,1)S(1)} async-done(((bf16[32,2,8,192]{3,2,1,0:T(8,128)(2,1)}), bf16[32,2,8,192]{3,2,1,0:T(8,128)(2,1)S(1)}, u32[]{:S(2)}, u32[]{:S(2)}) %all-to-all-start.1) | async-done | bytes 196640 | tf_op jit(solution)/shard_map/all_to_all | solution.py:11
  125.0 0.6 broadcast_in_dim.10
  125.6 8.4 %all-to-all-start.5 = ((f32[16,1,256]{2,1,0:T(1,128)}), f32[16,1,256]{2,1,0:T(1,128)}, u32[]{:S(2)}, u32[]{:S(2)}) async-start(f32[16,1,256]{2,1,0:T(1,128)} %broadcast_in_dim.10), calls=%async_computation.5 | async-start | bytes 32768 | tf_op jit(solution)/shard_map/all_to_all | solution.py:15
  134.5 1.9 fusion.11
  136.4 0.7 fusion.2
  137.1 1.3 reshape.209
  138.4 2.9 %all-to-all-done.5 = f32[16,1,256]{2,1,0:T(1,128)} async-done(((f32[16,1,256]{2,1,0:T(1,128)}), f32[16,1,256]{2,1,0:T(1,128)}, u32[]{:S(2)}, u32[]{:S(2)}) %all-to-all-start.5) | async-done | bytes 16416 | tf_op jit(solution)/shard_map/all_to_all | solution.py:15
  141.3 4.2 %all-to-all-start.4 = ((f32[32,6,1536]{2,1,0:T(8,128)}), f32[32,6,1536]{2,1,0:T(8,128)S(1)}, u32[]{:S(2)}, u32[]{:S(2)}) async-start(f32[32,6,1536]{2,1,0:T(8,128)} %reshape.209), calls=%async_computation.4 | async-start | bytes 3145728 | tf_op jit(solution)/shard_map/all_to_all | solution.py:11
  146.4 0.3 copy.167
  146.7 1.5 copy.154
  148.2 33.8 %all-to-all-done.4 = f32[32,6,1536]{2,1,0:T(8,128)S(1)} async-done(((f32[32,6,1536]{2,1,0:T(8,128)}), f32[32,6,1536]{2,1,0:T(8,128)S(1)}, u32[]{:S(2)}, u32[]{:S(2)}) %all-to-all-start.4) | async-done | bytes 1179680 | tf_op jit(solution)/shard_map/all_to_all | solution.py:11
  182.1 7.8 %all-to-all-start.7 = ((f32[16,1,10240]{2,1,0:T(1,128)}), f32[16,1,10240]{2,1,0:T(1,128)S(1)}, u32[]{:S(2)}, u32[]{:S(2)}) async-start(f32[16,1,10240]{2,1,0:T(1,128)} %copy.154), calls=%async_computation.7 | async-start | bytes 1310720 | tf_op jit(solution)/shard_map/all_to_all | solution.py:15
  189.9 0.8 reduce_sum.38
  190.8 19.0 %all-to-all-done.7 = f32[16,1,10240]{2,1,0:T(1,128)S(1)} async-done(((f32[16,1,10240]{2,1,0:T(1,128)}), f32[16,1,10240]{2,1,0:T(1,128)S(1)}, u32[]{:S(2)}, u32[]{:S(2)}) %all-to-all-start.7) | async-done | bytes 655392 | tf_op jit(solution)/shard_map/all_to_all | solution.py:15
  209.9 1.7 broadcast_in_dim.11
  211.5 5.3 %all-to-all-start.6 = ((f32[32,1,9472]{2,1,0:T(1,128)}), f32[32,1,9472]{2,1,0:T(1,128)S(1)}, u32[]{:S(2)}, u32[]{:S(2)}) async-start(f32[32,1,9472]{2,1,0:T(1,128)} %broadcast_in_dim.11), calls=%async_computation.6 | async-start | bytes 2424832 | tf_op jit(solution)/shard_map/all_to_all | solution.py:11
  217.5 0.9 fusion.39
  218.4 0.4 reduce_sum.39
  218.8 0.6 reshape.216
  219.4 0.7 reshape.217
  220.1 28.2 %all-to-all-done.6 = f32[32,1,9472]{2,1,0:T(1,128)S(1)} async-done(((f32[32,1,9472]{2,1,0:T(1,128)}), f32[32,1,9472]{2,1,0:T(1,128)S(1)}, u32[]{:S(2)}, u32[]{:S(2)}) %all-to-all-start.6) | async-done | bytes 1212448 | tf_op jit(solution)/shard_map/all_to_all | solution.py:11
  248.6 0.9 slice.101
  249.5 0.9 slice.99
  250.5 0.9 fusion.38
  (95 shorter events, 5.6 us)
Async XLA Ops:
  7.2 54.6 %copy-start = (bf16[96,1536]{1,0:T(8,128)(2,1)S(1)}, bf16[96,1536]{1,0:T(8,128)(2,1)}, u32[]{:S(2)}) copy-start(bf16[96,1536]{1,0:T(8,128)(2,1)} %param.10) | copy-start | bytes 884740
  7.2 52.2 %all-gather.2.cloned.1.call-start = ((), (), s32[]{:S(2)}) async-start(), calls=%async_computation.8 | async-start | bytes 2088960 | tf_op jit(solution)/shard_map/all_gather | solution.py:40
  9.7 52.1 %copy-start.16 = (bf16[96,512]{1,0:T(8,128)(2,1)S(1)}, bf16[96,512]{1,0:T(8,128)(2,1)}, u32[]{:S(2)}) copy-start(bf16[96,512]{1,0:T(8,128)(2,1)} %param.17) | copy-start | bytes 294916
  59.4 2.4 copy-start.1
  62.3 0.7 copy-start.17
  62.6 11.8 %copy-start.8 = (bf16[2,256,256]{2,1,0:T(8,128)(2,1)S(1)}, bf16[2,256,256]{2,1,0:T(8,128)(2,1)}, u32[]{:S(2)}) copy-start(bf16[2,256,256]{2,1,0:T(8,128)(2,1)} %param.12) | copy-start | bytes 786436
  63.8 18.2 %all-to-all-start.2 = ((f32[32,1,640]{2,1,0:T(1,128)}), f32[32,1,640]{2,1,0:T(1,128)S(1)}, u32[]{:S(2)}, u32[]{:S(2)}) async-start(f32[32,1,640]{2,1,0:T(1,128)} %all_to_all.39), calls=%async_computation.2 | async-start | bytes 163840 | tf_op jit(solution)/shard_map/all_to_all | solution.py:11
  74.4 0.6 copy-start.10
  74.4 11.5 %copy-start.13 = (s32[64]{0:T(128)S(1)}, s32[64]{0:T(128)}, u32[]{:S(2)}) copy-start(s32[64]{0:T(128)} %param.16) | copy-start | bytes 772
  75.0 28.3 %copy-start.9 = (bf16[8,64,64]{2,1,0:T(8,128)(2,1)S(1)}, bf16[8,64,64]{2,1,0:T(8,128)(2,1)}, u32[]{:S(2)}) copy-start(bf16[8,64,64]{2,1,0:T(8,128)(2,1)} %param.13) | copy-start | bytes 196612
  82.0 13.5 %all-to-all-start = ((bf16[32,2,8,192]{3,2,1,0:T(8,128)(2,1)}), bf16[32,2,8,192]{3,2,1,0:T(8,128)(2,1)S(1)}, u32[]{:S(2)}, u32[]{:S(2)}) async-start(bf16[32,2,8,192]{3,2,1,0:T(8,128)(2,1)} %copy.133), calls=%async_computation | async-start | bytes 524288 | tf_op jit(solution)/shard_map/all_to_all | solution.py:11
  85.9 0.5 copy-start.14
  96.2 15.2 %all-to-all-start.3 = ((f32[32,1,640]{2,1,0:T(1,128)}), f32[32,1,640]{2,1,0:T(1,128)S(1)}, u32[]{:S(2)}, u32[]{:S(2)}) async-start(f32[32,1,640]{2,1,0:T(1,128)} %broadcast_in_dim.8), calls=%async_computation.3 | async-start | bytes 163840 | tf_op jit(solution)/shard_map/all_to_all | solution.py:11
  102.6 12.8 %copy-start.12 = (bf16[96,128]{1,0:T(8,128)(2,1)S(1)}, bf16[96,128]{1,0:T(8,128)(2,1)}, u32[]{:S(2)}) copy-start(bf16[96,128]{1,0:T(8,128)(2,1)} %param.15) | copy-start | bytes 73732
  102.7 0.7 copy-start.2
  102.8 0.7 copy-start.4
  111.4 13.6 %all-to-all-start.1 = ((bf16[32,2,8,192]{3,2,1,0:T(8,128)(2,1)}), bf16[32,2,8,192]{3,2,1,0:T(8,128)(2,1)S(1)}, u32[]{:S(2)}, u32[]{:S(2)}) async-start(bf16[32,2,8,192]{3,2,1,0:T(8,128)(2,1)} %pad_maximum_fusion.1), calls=%async_computation.1 | async-start | bytes 524288 | tf_op jit(solution)/shard_map/all_to_all | solution.py:11
  125.6 15.7 %all-to-all-start.5 = ((f32[16,1,256]{2,1,0:T(1,128)}), f32[16,1,256]{2,1,0:T(1,128)}, u32[]{:S(2)}, u32[]{:S(2)}) async-start(f32[16,1,256]{2,1,0:T(1,128)} %broadcast_in_dim.10), calls=%async_computation.5 | async-start | bytes 32768 | tf_op jit(solution)/shard_map/all_to_all | solution.py:15
  134.1 2.3 copy-start.6
  138.4 7.1 %copy-start.3 = (bf16[32,2,8,96]{3,1,0,2:T(2,128)(2,1)S(1)}, bf16[32,2,8,96]{3,1,0,2:T(2,128)(2,1)}, u32[]{:S(2)}) copy-start(bf16[32,2,8,96]{3,1,0,2:T(2,128)(2,1)} %copy-done.2) | copy-start | bytes 294916
  138.4 7.1 %copy-start.5 = (bf16[32,2,8,96]{3,1,0,2:T(2,128)(2,1)S(1)}, bf16[32,2,8,96]{3,1,0,2:T(2,128)(2,1)}, u32[]{:S(2)}) copy-start(bf16[32,2,8,96]{3,1,0,2:T(2,128)(2,1)} %copy-done.4) | copy-start | bytes 294916
  138.4 7.6 %copy-start.7 = (bf16[2,32,8,96]{3,2,0,1:T(8,128)(2,1)S(1)}, bf16[2,32,8,96]{3,2,0,1:T(8,128)(2,1)}, u32[]{:S(2)}) copy-start(bf16[2,32,8,96]{3,2,0,1:T(8,128)(2,1)} %copy-done.6) | copy-start | bytes 294916
  138.4 7.6 %copy-start.11 = (bf16[512,96]{0,1:T(8,128)(2,1)S(1)}, bf16[512,96]{0,1:T(8,128)(2,1)}, u32[]{:S(2)}) copy-start(bf16[512,96]{0,1:T(8,128)(2,1)} %copy-done.10) | copy-start | bytes 294916
  141.3 40.7 %all-to-all-start.4 = ((f32[32,6,1536]{2,1,0:T(8,128)}), f32[32,6,1536]{2,1,0:T(8,128)S(1)}, u32[]{:S(2)}, u32[]{:S(2)}) async-start(f32[32,6,1536]{2,1,0:T(8,128)} %reshape.209), calls=%async_computation.4 | async-start | bytes 3145728 | tf_op jit(solution)/shard_map/all_to_all | solution.py:11
  182.1 27.8 %all-to-all-start.7 = ((f32[16,1,10240]{2,1,0:T(1,128)}), f32[16,1,10240]{2,1,0:T(1,128)S(1)}, u32[]{:S(2)}, u32[]{:S(2)}) async-start(f32[16,1,10240]{2,1,0:T(1,128)} %copy.154), calls=%async_computation.7 | async-start | bytes 1310720 | tf_op jit(solution)/shard_map/all_to_all | solution.py:15
  190.8 26.1 %copy-start.15 = (f32[64]{0:T(128)S(1)}, f32[64]{0:T(128)}, u32[]{:S(2)}) copy-start(f32[64]{0:T(128)} %copy-done.14) | copy-start | bytes 772
  211.5 36.8 %all-to-all-start.6 = ((f32[32,1,9472]{2,1,0:T(1,128)}), f32[32,1,9472]{2,1,0:T(1,128)S(1)}, u32[]{:S(2)}, u32[]{:S(2)}) async-start(f32[32,1,9472]{2,1,0:T(1,128)} %broadcast_in_dim.11), calls=%async_computation.6 | async-start | bytes 2424832 | tf_op jit(solution)/shard_map/all_to_all | solution.py:11
Sparse Core Ops, SparseCore 0:
  10.7 48.6 all-gather.1

commit v2 on v1

--- a/solution.py
+++ b/solution.py
@@ -13,6 +13,17 @@
 
 def chan_exchange(x):
     return lax.all_to_all(x, "chan", 0, 0, tiled=True)
+
+
+def split_hi_lo(x):
+    hi = x.astype(jnp.bfloat16)
+    lo = (x - hi.astype(jnp.float32)).astype(jnp.bfloat16)
+    return jnp.concatenate([hi, lo], axis=-1)
+
+
+def join_hi_lo(x):
+    n = x.shape[-1] // 2
+    return x[..., :n].astype(jnp.float32) + x[..., n:].astype(jnp.float32)
 
 
 def body(
@@ -73,9 +84,8 @@
 
     inner_send = inner_mix.reshape(blocks_here, n_seq, k_here, chan_rows).transpose(1, 0, 2, 3)
     d_send = d_mixed_bf.reshape(chan_rows, blocks_here, n_seq, k_here).transpose(2, 1, 3, 0)
-    recv2 = seq_exchange(jnp.concatenate([inner_send, d_send], axis=3))
-    columns = recv2[..., :chan_rows].reshape(n_seq * blocks_here, k_here, chan_rows)
-    d_outer = recv2[..., chan_rows:].reshape(n_seq * blocks_here, k_here, chan_rows)
+    mix_send = jnp.concatenate([inner_send, d_send], axis=3).reshape(n_seq, -1)
+    n_mix = mix_send.shape[1]
 
     small_send = jnp.concatenate(
         [
@@ -89,7 +99,11 @@
         ],
         axis=1,
     )
-    small_red = jnp.sum(seq_exchange(small_send), axis=0)
+    recv2 = seq_exchange(jnp.concatenate([mix_send, split_hi_lo(small_send)], axis=1))
+    mix2 = recv2[:, :n_mix].reshape(n_seq, blocks_here, k_here, 2 * chan_rows)
+    columns = mix2[..., :chan_rows].reshape(n_seq * blocks_here, k_here, chan_rows)
+    d_outer = mix2[..., chan_rows:].reshape(n_seq * blocks_here, k_here, chan_rows)
+    small_red = jnp.sum(join_hi_lo(recv2[:, n_mix:]), axis=0)
     n_a = docs_here * lat
     n_b = chan_rows * docs_here
     scale_here = lax.dynamic_slice(len_scale, (me * docs_here,), (docs_here,))
@@ -99,9 +113,6 @@
 
     up_float = up_latent.astype(jnp.float32)
     g_part = jnp.einsum("cd,cl->dl", per_doc_here, up_float, precision=HIGHEST)
-    g_here = jnp.sum(
-        chan_exchange(jnp.broadcast_to(g_part.reshape(1, n_a), (n_chan, n_a))), axis=0
-    )
 
     outer_mix = jnp.einsum(
         "kmi,ikc->mkc", second_factor, columns, preferred_element_type=jnp.float32
@@ -115,17 +126,22 @@
 
     outer_send = outer_mix.reshape(n_seq, blocks_here, k_here, chan_rows)
     dinner_send = d_inner.reshape(n_seq, blocks_here, k_here, chan_rows)
-    recv3 = seq_exchange(jnp.concatenate([outer_send, dinner_send], axis=3))
+    piece = jnp.concatenate(
+        [pooled_here.reshape(n_a), per_doc_here.reshape(n_b), xdoc_here.reshape(n_b)]
+    )
+    piece_b = jnp.broadcast_to(split_hi_lo(piece)[None, :], (n_seq, 2 * piece.shape[0]))
+    send3 = jnp.concatenate(
+        [jnp.concatenate([outer_send, dinner_send], axis=3).reshape(n_seq, -1), piece_b], axis=1
+    )
+    recv3_all = seq_exchange(send3)
+    recv3 = recv3_all[:, :n_mix].reshape(n_seq, blocks_here, k_here, 2 * chan_rows)
+    gath3 = join_hi_lo(recv3_all[:, n_mix:])
     outer_tok = (
         recv3[..., :chan_rows].transpose(3, 1, 0, 2).reshape(chan_rows, tok_cols).astype(jnp.float32)
     )
     d_rows = recv3[..., chan_rows:].transpose(1, 0, 2, 3).reshape(
         blocks_here, n_seq * k_here, chan_rows
     )
-    piece = jnp.concatenate(
-        [pooled_here.reshape(n_a), per_doc_here.reshape(n_b), xdoc_here.reshape(n_b)]
-    )
-    gath3 = seq_exchange(jnp.broadcast_to(piece[None, :], (n_seq, piece.shape[0])))
     pooled = gath3[:, :n_a].reshape(n_doc, lat)
     per_doc = (
         gath3[:, n_a : n_a + n_b].reshape(n_seq, chan_rows, docs_here).transpose(1, 0, 2)
@@ -164,10 +180,15 @@
     second_send = (
         d_second_part.reshape(k_here, n_chan, m_part, n_blk2).transpose(1, 0, 2, 3).reshape(n_chan, -1)
     )
-    fac_red = jnp.sum(chan_exchange(jnp.concatenate([first_send, second_send], axis=1)), axis=0)
+    g_send = jnp.broadcast_to(g_part.reshape(1, n_a), (n_chan, n_a))
+    fac_red = jnp.sum(
+        chan_exchange(jnp.concatenate([first_send, second_send, g_send], axis=1)), axis=0
+    )
     n_f = blocks_here * k_part * block_width
     d_first = fac_red[:n_f].reshape(blocks_here, k_part, block_width)
-    d_second = fac_red[n_f:].reshape(k_here, m_part, n_blk2)
+    n_s = k_here * m_part * n_blk2
+    d_second = fac_red[n_f : n_f + n_s].reshape(k_here, m_part, n_blk2)
+    g_here = fac_red[n_f + n_s :]
 
     piece5 = jnp.concatenate([proj_red.reshape(-1), g_here])
     gath5 = seq_exchange(jnp.broadcast_to(piece5[None, :], (n_seq, piece5.shape[0])))

time: 259 us -> 229 us (0.88); the launches traced: 258 us -> 225 us
  waiting for transfers between devices: 162 us -> 145 us
  starting transfers between devices: 49 us -> 33.7 us
    all_to_all x6 -> x4, waiting for transfers between devices: 92.6 us -> 82.1 us  [seq_exchange(): return lax.all_to_all(x, 'seq', 0, 0, tiled=True)]
    all_to_all x2 -> x1, starting transfers between devices: 16.2 us -> 7.84 us  [chan_exchange(): return lax.all_to_all(x, 'chan', 0, 0, tiled=True)]
    all_to_all x6 -> x4, starting transfers between devices: 32.8 us -> 25.8 us  [seq_exchange(): return lax.all_to_all(x, 'seq', 0, 0, tiled=True)]
    all_to_all x2 -> x1, waiting for transfers between devices: 21.9 us -> 15.3 us  [chan_exchange(): return lax.all_to_all(x, 'chan', 0, 0, tiled=True)]
  transfers between devices with their start and end apart: 9 -> 6, of which waited for: 9 -> 6; matrix products, arithmetic and copies ran while one was open for 7% -> 5% of each run, Pallas kernels for 0% -> 0%
where the time goes in v2:
time: 229 us; the launch traced here: 225 us
  waiting for transfers between devices  145 us (63%)
  starting transfers between devices  33.7 us (15%)
  local copies, waits for them, and re-layouts  15.3 us (7%)
  between operations  14.6 us (6%)
  matrix products  10.8 us (5%)
  other arithmetic  5.45 us (2%)
    all_to_all x4, waiting for transfers between devices, seq_exchange(): return lax.all_to_all(x, 'seq', 0, 0, tiled=True)  82.1 us
    all_gather x1, waiting for transfers between devices, body(): gathered_all = lax.all_gather(packed, 'chan', axis=0, tiled=True)  47.7 us
    all_to_all x4, starting transfers between devices, seq_exchange(): return lax.all_to_all(x, 'seq', 0, 0, tiled=True)  25.8 us
    all_to_all x1, waiting for transfers between devices, chan_exchange(): return lax.all_to_all(x, 'chan', 0, 0, tiled=True)  15.3 us
    all_to_all x1, starting transfers between devices, chan_exchange(): return lax.all_to_all(x, 'chan', 0, 0, tiled=True)  7.84 us
  transfers between devices with their start and end apart: 6, of which 6 were waited for; matrix products, arithmetic and copies ran while one was open for 5% of the time, Pallas kernels for 0%

profile of v2, /device:TPU:1, one launch (start us, length us, event | category | flops | bytes accessed | tf_op | source)
XLA Modules:
  0.0 224.9 jit_solution(8806900425481684672)
XLA Ops:
  7.2 1.6 pad_maximum_fusion.2
  8.9 0.7 copy.86
  9.8 0.7 sub.12
  10.5 1.1 fusion.27
  11.8 47.7 %all-gather.2.cloned.1.call-done = bf16[1536,640]{1,0:T(8,128)(2,1)} async-done(((bf16[96,640]{1,0:T(8,128)(2,1)}), bf16[1536,640]{1,0:T(8,128)(2,1)}) %all-gather.2.cloned.1.call-update) | async-done | bytes 1966096 | tf_op jit(solution)/shard_map/all_gather | solution.py:51
  59.4 2.0 fusion.17
  61.4 0.3 fusion.16
  61.9 0.4 fusion.4
  62.3 0.3 fusion.33
  62.9 0.4 convolution_convert_fusion.2
  63.3 0.2 fusion
  63.9 0.2 reshape.196
  64.2 0.5 broadcast.29
  64.7 0.8 reduce.2
  65.5 0.8 reshape.232
  66.2 9.3 %all-to-all-start = ((bf16[32,2,2176]{2,1,0:T(2,128)(2,1)}), bf16[32,2,2176]{2,1,0:T(2,128)(2,1)S(1)}, u32[]{:S(2)}, u32[]{:S(2)}) async-start(bf16[32,2,2176]{2,1,0:T(2,128)(2,1)} %reshape.232), calls=%async_computation | async-start | bytes 557056 | tf_op jit(solution)/shard_map/all_to_all | solution.py:11
  75.6 10.0 %all-to-all-done = bf16[32,2,2176]{2,1,0:T(2,128)(2,1)S(1)} async-done(((bf16[32,2,2176]{2,1,0:T(2,128)(2,1)}), bf16[32,2,2176]{2,1,0:T(2,128)(2,1)S(1)}, u32[]{:S(2)}, u32[]{:S(2)}) %all-to-all-start) | async-done | bytes 278560 | tf_op jit(solution)/shard_map/all_to_all | solution.py:11
  85.7 0.2 reshape.233
  86.1 0.3 reshape.204
  86.6 0.2 convolution_convert_fusion.1
  87.6 0.3 reshape.209
  88.0 0.8 reduce.3
  88.8 0.8 reshape.234
  89.6 6.8 %all-to-all-start.1 = ((bf16[32,2,2176]{2,1,0:T(2,128)(2,1)}), bf16[32,2,2176]{2,1,0:T(2,128)(2,1)S(1)}, u32[]{:S(2)}, u32[]{:S(2)}) async-start(bf16[32,2,2176]{2,1,0:T(2,128)(2,1)} %reshape.234), calls=%async_computation.1 | async-start | bytes 557056 | tf_op jit(solution)/shard_map/all_to_all | solution.py:11
  96.6 0.2 reshape.220
  97.2 8.8 %all-to-all-done.1 = bf16[32,2,2176]{2,1,0:T(2,128)(2,1)S(1)} async-done(((bf16[32,2,2176]{2,1,0:T(2,128)(2,1)}), bf16[32,2,2176]{2,1,0:T(2,128)(2,1)S(1)}, u32[]{:S(2)}, u32[]{:S(2)}) %all-to-all-start.1) | async-done | bytes 278560 | tf_op jit(solution)/shard_map/all_to_all | solution.py:11
  106.1 0.2 reshape.235
  106.4 0.3 reshape.211
  107.0 0.3 copy.120
  107.4 1.5 copy.107
  109.0 7.8 %all-to-all-start.3 = ((f32[16,1,10496]{2,1,0:T(1,128)}), f32[16,1,10496]{2,1,0:T(1,128)S(1)}, u32[]{:S(2)}, u32[]{:S(2)}) async-start(f32[16,1,10496]{2,1,0:T(1,128)} %copy.107), calls=%async_computation.3 | async-start | bytes 1343488 | tf_op jit(solution)/shard_map/all_to_all | solution.py:15
  117.0 0.2 fusion.1
  117.4 1.0 fusion.11
  118.4 2.1 fusion.2
  120.5 1.3 reshape.215
  121.8 15.3 %all-to-all-done.3 = f32[16,1,10496]{2,1,0:T(1,128)S(1)} async-done(((f32[16,1,10496]{2,1,0:T(1,128)}), f32[16,1,10496]{2,1,0:T(1,128)S(1)}, u32[]{:S(2)}, u32[]{:S(2)}) %all-to-all-start.3) | async-done | bytes 671776 | tf_op jit(solution)/shard_map/all_to_all | solution.py:15
  137.1 4.3 %all-to-all-start.2 = ((f32[32,6,1536]{2,1,0:T(8,128)}), f32[32,6,1536]{2,1,0:T(8,128)S(1)}, u32[]{:S(2)}, u32[]{:S(2)}) async-start(f32[32,6,1536]{2,1,0:T(8,128)} %reshape.215), calls=%async_computation.2 | async-start | bytes 3145728 | tf_op jit(solution)/shard_map/all_to_all | solution.py:11
  141.4 0.4 reduce_sum.29
  141.8 38.2 %all-to-all-done.2 = f32[32,6,1536]{2,1,0:T(8,128)S(1)} async-done(((f32[32,6,1536]{2,1,0:T(8,128)}), f32[32,6,1536]{2,1,0:T(8,128)S(1)}, u32[]{:S(2)}, u32[]{:S(2)}) %all-to-all-start.2) | async-done | bytes 1179680 | tf_op jit(solution)/shard_map/all_to_all | solution.py:11
  180.1 1.7 broadcast_in_dim.11
  181.8 5.5 %all-to-all-start.4 = ((f32[32,1,9472]{2,1,0:T(1,128)}), f32[32,1,9472]{2,1,0:T(1,128)S(1)}, u32[]{:S(2)}, u32[]{:S(2)}) async-start(f32[32,1,9472]{2,1,0:T(1,128)} %broadcast_in_dim.11), calls=%async_computation.4 | async-start | bytes 2424832 | tf_op jit(solution)/shard_map/all_to_all | solution.py:11
  187.8 0.9 fusion.41
  188.7 0.6 reshape.222
  189.3 0.7 reshape.223
  190.0 25.0 %all-to-all-done.4 = f32[32,1,9472]{2,1,0:T(1,128)S(1)} async-done(((f32[32,1,9472]{2,1,0:T(1,128)}), f32[32,1,9472]{2,1,0:T(1,128)S(1)}, u32[]{:S(2)}, u32[]{:S(2)}) %all-to-all-start.4) | async-done | bytes 1212448 | tf_op jit(solution)/shard_map/all_to_all | solution.py:11
  215.2 0.9 slice.133
  216.2 0.9 slice.135
  217.2 0.9 fusion.40
  (87 shorter events, 4.8 us)
Async XLA Ops:
  7.2 52.2 %copy-start = (bf16[96,1536]{1,0:T(8,128)(2,1)S(1)}, bf16[96,1536]{1,0:T(8,128)(2,1)}, u32[]{:S(2)}) copy-start(bf16[96,1536]{1,0:T(8,128)(2,1)} %param.10) | copy-start | bytes 884740
  7.2 52.2 %all-gather.2.cloned.1.call-start = ((), (), s32[]{:S(2)}) async-start(), calls=%async_computation.5 | async-start | bytes 2088960 | tf_op jit(solution)/shard_map/all_gather | solution.py:51
  11.8 49.6 %copy-start.7 = (bf16[96,512]{1,0:T(8,128)(2,1)S(1)}, bf16[96,512]{1,0:T(8,128)(2,1)}, u32[]{:S(2)}) copy-start(bf16[96,512]{1,0:T(8,128)(2,1)} %param.17) | copy-start | bytes 294916
  59.4 2.5 %copy-start.1 = (bf16[1536,640]{1,0:T(8,128)(2,1)S(1)}, bf16[1536,640]{1,0:T(8,128)(2,1)}, u32[]{:S(2)}) copy-start(bf16[1536,640]{1,0:T(8,128)(2,1)} %all-gather.2.cloned.1.call-done) | copy-start | bytes 5898244
  61.9 1.0 copy-start.6
  62.3 1.0 copy-start.2
  63.8 11.7 %copy-start.5 = (s32[64]{0:T(128)S(1)}, s32[64]{0:T(128)}, u32[]{:S(2)}) copy-start(s32[64]{0:T(128)} %param.16) | copy-start | bytes 772
  66.2 19.4 %all-to-all-start = ((bf16[32,2,2176]{2,1,0:T(2,128)(2,1)}), bf16[32,2,2176]{2,1,0:T(2,128)(2,1)S(1)}, u32[]{:S(2)}, u32[]{:S(2)}) async-start(bf16[32,2,2176]{2,1,0:T(2,128)(2,1)} %reshape.232), calls=%async_computation | async-start | bytes 557056 | tf_op jit(solution)/shard_map/all_to_all | solution.py:11
  75.6 11.0 %copy-start.3 = (bf16[8,64,64]{2,1,0:T(8,128)(2,1)S(1)}, bf16[8,64,64]{2,1,0:T(8,128)(2,1)}, u32[]{:S(2)}) copy-start(bf16[8,64,64]{2,1,0:T(8,128)(2,1)} %param.13) | copy-start | bytes 196612
  88.0 9.0 %copy-start.4 = (bf16[96,128]{1,0:T(8,128)(2,1)S(1)}, bf16[96,128]{1,0:T(8,128)(2,1)}, u32[]{:S(2)}) copy-start(bf16[96,128]{1,0:T(8,128)(2,1)} %param.15) | copy-start | bytes 73732
  89.6 16.5 %all-to-all-start.1 = ((bf16[32,2,2176]{2,1,0:T(2,128)(2,1)}), bf16[32,2,2176]{2,1,0:T(2,128)(2,1)S(1)}, u32[]{:S(2)}, u32[]{:S(2)}) async-start(bf16[32,2,2176]{2,1,0:T(2,128)(2,1)} %reshape.234), calls=%async_computation.1 | async-start | bytes 557056 | tf_op jit(solution)/shard_map/all_to_all | solution.py:11
  109.0 28.1 %all-to-all-start.3 = ((f32[16,1,10496]{2,1,0:T(1,128)}), f32[16,1,10496]{2,1,0:T(1,128)S(1)}, u32[]{:S(2)}, u32[]{:S(2)}) async-start(f32[16,1,10496]{2,1,0:T(1,128)} %copy.107), calls=%async_computation.3 | async-start | bytes 1343488 | tf_op jit(solution)/shard_map/all_to_all | solution.py:15
  137.1 42.9 %all-to-all-start.2 = ((f32[32,6,1536]{2,1,0:T(8,128)}), f32[32,6,1536]{2,1,0:T(8,128)S(1)}, u32[]{:S(2)}, u32[]{:S(2)}) async-start(f32[32,6,1536]{2,1,0:T(8,128)} %reshape.215), calls=%async_computation.2 | async-start | bytes 3145728 | tf_op jit(solution)/shard_map/all_to_all | solution.py:11
  181.8 33.2 %all-to-all-start.4 = ((f32[32,1,9472]{2,1,0:T(1,128)}), f32[32,1,9472]{2,1,0:T(1,128)S(1)}, u32[]{:S(2)}, u32[]{:S(2)}) async-start(f32[32,1,9472]{2,1,0:T(1,128)} %broadcast_in_dim.11), calls=%async_computation.4 | async-start | bytes 2424832 | tf_op jit(solution)/shard_map/all_to_all | solution.py:11
Sparse Core Ops, SparseCore 0:
  10.7 48.6 all-gather.1

commit v3 on v2

--- a/solution.py
+++ b/solution.py
@@ -16,9 +16,9 @@
 
 
 def split_hi_lo(x):
-    hi = x.astype(jnp.bfloat16)
-    lo = (x - hi.astype(jnp.float32)).astype(jnp.bfloat16)
-    return jnp.concatenate([hi, lo], axis=-1)
+    hi = lax.reduce_precision(x, exponent_bits=8, mantissa_bits=7)
+    lo = x - hi
+    return jnp.concatenate([hi.astype(jnp.bfloat16), lo.astype(jnp.bfloat16)], axis=-1)
 
 
 def join_hi_lo(x):
@@ -169,7 +169,8 @@
     rows_here = 2 * chan_rows // n_seq
     width = d_proj_part.shape[1]
 
-    proj_red = jnp.sum(seq_exchange(d_proj_part.reshape(n_seq, rows_here, width)), axis=0)
+    proj_send = d_proj_part.reshape(n_seq, rows_here, width).astype(jnp.bfloat16)
+    proj_red = jnp.sum(seq_exchange(proj_send).astype(jnp.float32), axis=0)
     k_part = block_width // n_chan
     m_part = n_blk2 // n_chan
     first_send = (

time: 229 us -> 215 us (0.939); the launches traced: 225 us -> 215 us
  waiting for transfers between devices: 145 us -> 132 us
  starting transfers between devices: 33.7 us -> 36.4 us
    all_to_all x4, waiting for transfers between devices: 82.1 us -> 64.3 us  [seq_exchange(): return lax.all_to_all(x, 'seq', 0, 0, tiled=True)]
    all_to_all x1, waiting for transfers between devices: 15.3 us -> 20.1 us  [chan_exchange(): return lax.all_to_all(x, 'chan', 0, 0, tiled=True)]
  transfers between devices with their start and end apart: 6 -> 6, of which waited for: 6 -> 6; matrix products, arithmetic and copies ran while one was open for 5% -> 4% of each run, Pallas kernels for 0% -> 0%
where the time goes in v3:
time: 215 us
  waiting for transfers between devices  132 us (61%)
  starting transfers between devices  36.4 us (17%)
  local copies, waits for them, and re-layouts  15.1 us (7%)
  between operations  14.7 us (7%)
  matrix products  10.9 us (5%)
  other arithmetic  5.46 us (3%)
    all_to_all x4, waiting for transfers between devices, seq_exchange(): return lax.all_to_all(x, 'seq', 0, 0, tiled=True)  64.3 us
    all_gather x1, waiting for transfers between devices, body(): gathered_all = lax.all_gather(packed, 'chan', axis=0, tiled=True)  47.6 us
    all_to_all x4, starting transfers between devices, seq_exchange(): return lax.all_to_all(x, 'seq', 0, 0, tiled=True)  27.1 us
    all_to_all x1, waiting for transfers between devices, chan_exchange(): return lax.all_to_all(x, 'chan', 0, 0, tiled=True)  20.1 us
    all_to_all x1, starting transfers between devices, chan_exchange(): return lax.all_to_all(x, 'chan', 0, 0, tiled=True)  9.25 us
  transfers between devices with their start and end apart: 6, of which 6 were waited for; matrix products, arithmetic and copies ran while one was open for 4% of the time, Pallas kernels for 0%

profile of v3, /device:TPU:1, one launch (start us, length us, event | category | flops | bytes accessed | tf_op | source)
XLA Modules:
  0.0 214.6 jit_solution(18446473755201916711)
XLA Ops:
  7.2 1.6 pad_maximum_fusion.2
  8.9 0.7 copy.86
  9.9 0.7 sub.12
  10.5 1.1 fusion.27
  11.8 47.6 %all-gather.2.cloned.1.call-done = bf16[1536,640]{1,0:T(8,128)(2,1)} async-done(((bf16[96,640]{1,0:T(8,128)(2,1)}), bf16[1536,640]{1,0:T(8,128)(2,1)}) %all-gather.2.cloned.1.call-update) | async-done | bytes 1966096 | tf_op jit(solution)/shard_map/all_gather | solution.py:51
  59.4 2.0 convolution_convert_fusion.3
  61.4 0.2 fusion
  61.8 0.4 fusion.3
  62.2 0.3 fusion.32
  62.5 0.4 fusion.16
  63.3 0.3 reshape.195
  63.5 0.3 fusion.15
  64.2 0.5 broadcast.29
  64.7 0.8 reduce.2
  65.5 0.8 reshape.230
  66.3 9.3 %all-to-all-start = ((bf16[32,2,2176]{2,1,0:T(2,128)(2,1)}), bf16[32,2,2176]{2,1,0:T(2,128)(2,1)S(1)}, u32[]{:S(2)}, u32[]{:S(2)}) async-start(bf16[32,2,2176]{2,1,0:T(2,128)(2,1)} %reshape.230), calls=%async_computation | async-start | bytes 557056 | tf_op jit(solution)/shard_map/all_to_all | solution.py:11
  75.6 10.0 %all-to-all-done = bf16[32,2,2176]{2,1,0:T(2,128)(2,1)S(1)} async-done(((bf16[32,2,2176]{2,1,0:T(2,128)(2,1)}), bf16[32,2,2176]{2,1,0:T(2,128)(2,1)S(1)}, u32[]{:S(2)}, u32[]{:S(2)}) %all-to-all-start) | async-done | bytes 278560 | tf_op jit(solution)/shard_map/all_to_all | solution.py:11
  85.7 0.2 reshape.231
  86.1 0.3 reshape.203
  87.1 0.2 convolution_convert_fusion.2
  87.6 0.3 reshape.208
  88.0 0.8 reduce.3
  88.8 0.8 reshape.232
  89.6 6.8 %all-to-all-start.1 = ((bf16[32,2,2176]{2,1,0:T(2,128)(2,1)}), bf16[32,2,2176]{2,1,0:T(2,128)(2,1)S(1)}, u32[]{:S(2)}, u32[]{:S(2)}) async-start(bf16[32,2,2176]{2,1,0:T(2,128)(2,1)} %reshape.232), calls=%async_computation.1 | async-start | bytes 557056 | tf_op jit(solution)/shard_map/all_to_all | solution.py:11
  96.8 0.2 reshape.218
  97.2 8.8 %all-to-all-done.1 = bf16[32,2,2176]{2,1,0:T(2,128)(2,1)S(1)} async-done(((bf16[32,2,2176]{2,1,0:T(2,128)(2,1)}), bf16[32,2,2176]{2,1,0:T(2,128)(2,1)S(1)}, u32[]{:S(2)}, u32[]{:S(2)}) %all-to-all-start.1) | async-done | bytes 278560 | tf_op jit(solution)/shard_map/all_to_all | solution.py:11
  106.1 0.2 reshape.233
  106.4 0.3 reshape.210
  106.8 0.2 fusion.1
  107.6 1.0 fusion.10
  108.6 2.1 convolution_convert_fusion
  110.7 1.1 convert_element_type.130
  111.8 6.4 %all-to-all-start.2 = ((bf16[32,6,1536]{2,1,0:T(8,128)(2,1)}), bf16[32,6,1536]{2,1,0:T(8,128)(2,1)S(1)}, u32[]{:S(2)}, u32[]{:S(2)}) async-start(bf16[32,6,1536]{2,1,0:T(8,128)(2,1)} %convert_element_type.130), calls=%async_computation.2 | async-start | bytes 1572864 | tf_op jit(solution)/shard_map/all_to_all | solution.py:11
  118.3 0.3 copy.120
  118.6 1.6 copy.107
  120.2 16.8 %all-to-all-done.2 = bf16[32,6,1536]{2,1,0:T(8,128)(2,1)S(1)} async-done(((bf16[32,6,1536]{2,1,0:T(8,128)(2,1)}), bf16[32,6,1536]{2,1,0:T(8,128)(2,1)S(1)}, u32[]{:S(2)}, u32[]{:S(2)}) %all-to-all-start.2) | async-done | bytes 589856 | tf_op jit(solution)/shard_map/all_to_all | solution.py:11
  137.0 9.3 %all-to-all-start.3 = ((f32[16,1,10496]{2,1,0:T(1,128)}), f32[16,1,10496]{2,1,0:T(1,128)S(1)}, u32[]{:S(2)}, u32[]{:S(2)}) async-start(f32[16,1,10496]{2,1,0:T(1,128)} %copy.107), calls=%async_computation.3 | async-start | bytes 1343488 | tf_op jit(solution)/shard_map/all_to_all | solution.py:15
  146.5 20.1 %all-to-all-done.3 = f32[16,1,10496]{2,1,0:T(1,128)S(1)} async-done(((f32[16,1,10496]{2,1,0:T(1,128)}), f32[16,1,10496]{2,1,0:T(1,128)S(1)}, u32[]{:S(2)}, u32[]{:S(2)}) %all-to-all-start.3) | async-done | bytes 671776 | tf_op jit(solution)/shard_map/all_to_all | solution.py:15
  166.6 0.4 reduce_sum.29
  167.0 1.7 broadcast_in_dim.11
  168.7 4.7 %all-to-all-start.4 = ((f32[32,1,9472]{2,1,0:T(1,128)}), f32[32,1,9472]{2,1,0:T(1,128)S(1)}, u32[]{:S(2)}, u32[]{:S(2)}) async-start(f32[32,1,9472]{2,1,0:T(1,128)} %broadcast_in_dim.11), calls=%async_computation.4 | async-start | bytes 2424832 | tf_op jit(solution)/shard_map/all_to_all | solution.py:11
  173.9 0.9 fusion.40
  174.8 0.6 reshape.220
  175.5 0.7 reshape.221
  176.1 28.6 %all-to-all-done.4 = f32[32,1,9472]{2,1,0:T(1,128)S(1)} async-done(((f32[32,1,9472]{2,1,0:T(1,128)}), f32[32,1,9472]{2,1,0:T(1,128)S(1)}, u32[]{:S(2)}, u32[]{:S(2)}) %all-to-all-start.4) | async-done | bytes 1212448 | tf_op jit(solution)/shard_map/all_to_all | solution.py:11
  205.0 0.9 slice.135
  206.0 0.9 slice.133
  206.9 0.9 fusion.39
  (83 shorter events, 4.8 us)
Async XLA Ops:
  7.2 55.3 %copy-start = (bf16[96,1536]{1,0:T(8,128)(2,1)S(1)}, bf16[96,1536]{1,0:T(8,128)(2,1)}, u32[]{:S(2)}) copy-start(bf16[96,1536]{1,0:T(8,128)(2,1)} %param.10) | copy-start | bytes 884740
  7.2 54.2 %copy-start.1 = (bf16[2,256,256]{2,1,0:T(8,128)(2,1)S(1)}, bf16[2,256,256]{2,1,0:T(8,128)(2,1)}, u32[]{:S(2)}) copy-start(bf16[2,256,256]{2,1,0:T(8,128)(2,1)} %param.12) | copy-start | bytes 786436
  7.2 52.2 %all-gather.2.cloned.1.call-start = ((), (), s32[]{:S(2)}) async-start(), calls=%async_computation.5 | async-start | bytes 2088960 | tf_op jit(solution)/shard_map/all_gather | solution.py:51
  59.4 2.4 %copy-start.5 = (bf16[1536,640]{1,0:T(8,128)(2,1)S(1)}, bf16[1536,640]{1,0:T(8,128)(2,1)}, u32[]{:S(2)}) copy-start(bf16[1536,640]{1,0:T(8,128)(2,1)} %all-gather.2.cloned.1.call-done) | copy-start | bytes 5898244
  61.4 1.1 copy-start.6
  63.8 11.7 %copy-start.4 = (s32[64]{0:T(128)S(1)}, s32[64]{0:T(128)}, u32[]{:S(2)}) copy-start(s32[64]{0:T(128)} %param.16) | copy-start | bytes 772
  66.3 19.4 %all-to-all-start = ((bf16[32,2,2176]{2,1,0:T(2,128)(2,1)}), bf16[32,2,2176]{2,1,0:T(2,128)(2,1)S(1)}, u32[]{:S(2)}, u32[]{:S(2)}) async-start(bf16[32,2,2176]{2,1,0:T(2,128)(2,1)} %reshape.230), calls=%async_computation | async-start | bytes 557056 | tf_op jit(solution)/shard_map/all_to_all | solution.py:11
  75.6 11.0 %copy-start.2 = (bf16[8,64,64]{2,1,0:T(8,128)(2,1)S(1)}, bf16[8,64,64]{2,1,0:T(8,128)(2,1)}, u32[]{:S(2)}) copy-start(bf16[8,64,64]{2,1,0:T(8,128)(2,1)} %param.13) | copy-start | bytes 196612
  88.0 9.0 %copy-start.3 = (bf16[96,128]{1,0:T(8,128)(2,1)S(1)}, bf16[96,128]{1,0:T(8,128)(2,1)}, u32[]{:S(2)}) copy-start(bf16[96,128]{1,0:T(8,128)(2,1)} %param.15) | copy-start | bytes 73732
  89.6 16.5 %all-to-all-start.1 = ((bf16[32,2,2176]{2,1,0:T(2,128)(2,1)}), bf16[32,2,2176]{2,1,0:T(2,128)(2,1)S(1)}, u32[]{:S(2)}, u32[]{:S(2)}) async-start(bf16[32,2,2176]{2,1,0:T(2,128)(2,1)} %reshape.232), calls=%async_computation.1 | async-start | bytes 557056 | tf_op jit(solution)/shard_map/all_to_all | solution.py:11
  111.8 25.2 %all-to-all-start.2 = ((bf16[32,6,1536]{2,1,0:T(8,128)(2,1)}), bf16[32,6,1536]{2,1,0:T(8,128)(2,1)S(1)}, u32[]{:S(2)}, u32[]{:S(2)}) async-start(bf16[32,6,1536]{2,1,0:T(8,128)(2,1)} %convert_element_type.130), calls=%async_computation.2 | async-start | bytes 1572864 | tf_op jit(solution)/shard_map/all_to_all | solution.py:11
  137.0 29.5 %all-to-all-start.3 = ((f32[16,1,10496]{2,1,0:T(1,128)}), f32[16,1,10496]{2,1,0:T(1,128)S(1)}, u32[]{:S(2)}, u32[]{:S(2)}) async-start(f32[16,1,10496]{2,1,0:T(1,128)} %copy.107), calls=%async_computation.3 | async-start | bytes 1343488 | tf_op jit(solution)/shard_map/all_to_all | solution.py:15
  168.7 36.0 %all-to-all-start.4 = ((f32[32,1,9472]{2,1,0:T(1,128)}), f32[32,1,9472]{2,1,0:T(1,128)S(1)}, u32[]{:S(2)}, u32[]{:S(2)}) async-start(f32[32,1,9472]{2,1,0:T(1,128)} %broadcast_in_dim.11), calls=%async_computation.4 | async-start | bytes 2424832 | tf_op jit(solution)/shard_map/all_to_all | solution.py:11
Sparse Core Ops, SparseCore 0:
  10.7 48.6 all-gather.1

commit v4 on v3

--- a/solution.py
+++ b/solution.py
@@ -127,7 +127,12 @@
     outer_send = outer_mix.reshape(n_seq, blocks_here, k_here, chan_rows)
     dinner_send = d_inner.reshape(n_seq, blocks_here, k_here, chan_rows)
     piece = jnp.concatenate(
-        [pooled_here.reshape(n_a), per_doc_here.reshape(n_b), xdoc_here.reshape(n_b)]
+        [
+            pooled_here.reshape(n_a),
+            per_doc_here.reshape(n_b),
+            xdoc_here.reshape(n_b),
+            g_part.reshape(n_a),
+        ]
     )
     piece_b = jnp.broadcast_to(split_hi_lo(piece)[None, :], (n_seq, 2 * piece.shape[0]))
     send3 = jnp.concatenate(
@@ -147,8 +152,9 @@
         gath3[:, n_a : n_a + n_b].reshape(n_seq, chan_rows, docs_here).transpose(1, 0, 2)
     ).reshape(chan_rows, n_doc)
     xdoc = (
-        gath3[:, n_a + n_b :].reshape(n_seq, chan_rows, docs_here).transpose(1, 0, 2)
+        gath3[:, n_a + n_b : n_a + 2 * n_b].reshape(n_seq, chan_rows, docs_here).transpose(1, 0, 2)
     ).reshape(chan_rows, n_doc)
+    g_gath = gath3[:, n_a + 2 * n_b :].reshape(1, n_doc * lat)
 
     spread = jnp.einsum("dl,cl->cd", pooled, up_float, precision=HIGHEST)
     summary = jnp.dot(spread, member, precision=HIGHEST)
@@ -181,21 +187,20 @@
     second_send = (
         d_second_part.reshape(k_here, n_chan, m_part, n_blk2).transpose(1, 0, 2, 3).reshape(n_chan, -1)
     )
-    g_send = jnp.broadcast_to(g_part.reshape(1, n_a), (n_chan, n_a))
-    fac_red = jnp.sum(
-        chan_exchange(jnp.concatenate([first_send, second_send, g_send], axis=1)), axis=0
-    )
+    g_send = jnp.broadcast_to(g_gath, (n_chan, n_doc * lat))
+    fac_send = jnp.concatenate([first_send, second_send, g_send], axis=1)
+    fac_red = lax.psum_scatter(
+        fac_send.reshape(-1, 128), "chan", scatter_dimension=0, tiled=True
+    ).reshape(-1)
     n_f = blocks_here * k_part * block_width
     d_first = fac_red[:n_f].reshape(blocks_here, k_part, block_width)
     n_s = k_here * m_part * n_blk2
     d_second = fac_red[n_f : n_f + n_s].reshape(k_here, m_part, n_blk2)
-    g_here = fac_red[n_f + n_s :]
-
-    piece5 = jnp.concatenate([proj_red.reshape(-1), g_here])
-    gath5 = seq_exchange(jnp.broadcast_to(piece5[None, :], (n_seq, piece5.shape[0])))
-    n_p = rows_here * width
-    d_proj = gath5[:, :n_p].reshape(2 * chan_rows, width)
-    d_pooled = gath5[:, n_p:].reshape(n_doc, lat) * len_scale[:, None]
+    g_full = fac_red[n_f + n_s :].reshape(n_doc, lat)
+
+    gath5 = seq_exchange(jnp.broadcast_to(proj_red[None], (n_seq, rows_here, width)))
+    d_proj = gath5.reshape(2 * chan_rows, width)
+    d_pooled = g_full * len_scale[:, None]
     d_down = jnp.einsum(
         "cd,dl->cl", xdoc, d_pooled.astype(jnp.bfloat16).astype(jnp.float32), precision=HIGHEST
     )

time: 215 us -> 201 us (0.935)
  waiting for transfers between devices: 132 us -> 117 us
  starting transfers between devices: 36.4 us -> 31.2 us
  matrix products: 10.9 us -> 14.5 us
    reduce_scatter x0 -> x1, waiting for transfers between devices: none -> 33.4 us  [body(): lax.psum_scatter(fac_send.reshape(-1, 128), 'chan', scatter_dimension=0,...]
    all_to_all x4, waiting for transfers between devices: 64.3 us -> 36.4 us  [seq_exchange(): return lax.all_to_all(x, 'seq', 0, 0, tiled=True)]
    all_to_all x1 -> x0, waiting for transfers between devices: 20.1 us -> none  [chan_exchange(): return lax.all_to_all(x, 'chan', 0, 0, tiled=True)]
    all_to_all x1 -> x0, starting transfers between devices: 9.25 us -> none  [chan_exchange(): return lax.all_to_all(x, 'chan', 0, 0, tiled=True)]
    all_to_all x4, starting transfers between devices: 27.1 us -> 31.1 us  [seq_exchange(): return lax.all_to_all(x, 'seq', 0, 0, tiled=True)]
  transfers between devices with their start and end apart: 6 -> 6, of which waited for: 6 -> 5; matrix products, arithmetic and copies ran while one was open for 4% -> 6% of each run, Pallas kernels for 0% -> 0%
where the time goes in v4:
time: 201 us; the launch traced here: 198 us
  waiting for transfers between devices  117 us (58%)
  starting transfers between devices  31.2 us (16%)
  local copies, waits for them, and re-layouts  15.6 us (8%)
  between operations  14.6 us (7%)
  matrix products  14.5 us (7%)
  other arithmetic  5.08 us (3%)
    all_gather x1, waiting for transfers between devices, body(): gathered_all = lax.all_gather(packed, 'chan', axis=0, tiled=True)  47.6 us
    all_to_all x4, waiting for transfers between devices, seq_exchange(): return lax.all_to_all(x, 'seq', 0, 0, tiled=True)  36.4 us
    reduce_scatter x1, waiting for transfers between devices, body(): lax.psum_scatter(fac_send.reshape(-1, 128), 'chan', scatter_dimension=0,...  33.4 us
    all_to_all x4, starting transfers between devices, seq_exchange(): return lax.all_to_all(x, 'seq', 0, 0, tiled=True)  31.1 us
  transfers between devices with their start and end apart: 6, of which 5 were waited for; matrix products, arithmetic and copies ran while one was open for 6% of the time, Pallas kernels for 0%

profile of v4, /device:TPU:1, one launch (start us, length us, event | category | flops | bytes accessed | tf_op | source)
XLA Modules:
  0.0 198.5 jit_solution(10429211262752419553)
XLA Ops:
  7.2 1.6 pad_maximum_fusion.2
  8.9 0.7 copy.85
  9.9 0.7 sub.12
  10.5 1.1 fusion.27
  11.8 47.6 %all-gather.2.cloned.1.call-done = bf16[1536,640]{1,0:T(8,128)(2,1)} async-done(((bf16[96,640]{1,0:T(8,128)(2,1)}), bf16[1536,640]{1,0:T(8,128)(2,1)}) %all-gather.2.cloned.1.call-update) | async-done | bytes 1966096 | tf_op jit(solution)/shard_map/all_gather | solution.py:51
  59.4 1.9 convolution_convert_fusion.3
  61.3 0.2 fusion
  61.7 2.0 fusion.3
  63.6 0.3 fusion.35
  63.9 1.8 fusion.16
  66.1 0.2 reshape.192
  66.3 0.3 fusion.15
  67.0 0.5 broadcast.29
  67.5 0.8 reduce.1
  68.3 0.8 reshape.228
  69.1 9.3 %all-to-all-start = ((bf16[32,2,2176]{2,1,0:T(2,128)(2,1)}), bf16[32,2,2176]{2,1,0:T(2,128)(2,1)S(1)}, u32[]{:S(2)}, u32[]{:S(2)}) async-start(bf16[32,2,2176]{2,1,0:T(2,128)(2,1)} %reshape.228), calls=%async_computation | async-start | bytes 557056 | tf_op jit(solution)/shard_map/all_to_all | solution.py:11
  78.4 10.1 %all-to-all-done = bf16[32,2,2176]{2,1,0:T(2,128)(2,1)S(1)} async-done(((bf16[32,2,2176]{2,1,0:T(2,128)(2,1)}), bf16[32,2,2176]{2,1,0:T(2,128)(2,1)S(1)}, u32[]{:S(2)}, u32[]{:S(2)}) %all-to-all-start) | async-done | bytes 278560 | tf_op jit(solution)/shard_map/all_to_all | solution.py:11
  88.5 0.2 reshape.229
  89.1 0.3 reshape.200
  90.1 0.2 convolution_convert_fusion.2
  90.6 0.3 reshape.205
  91.2 0.8 reduce.2
  92.0 0.8 reshape.230
  92.8 6.8 %all-to-all-start.1 = ((bf16[32,2,2432]{2,1,0:T(2,128)(2,1)}), bf16[32,2,2432]{2,1,0:T(2,128)(2,1)S(1)}, u32[]{:S(2)}, u32[]{:S(2)}) async-start(bf16[32,2,2432]{2,1,0:T(2,128)(2,1)} %reshape.230), calls=%async_computation.1 | async-start | bytes 622592 | tf_op jit(solution)/shard_map/all_to_all | solution.py:11
  99.8 0.2 reshape.216
  100.1 9.4 %all-to-all-done.1 = bf16[32,2,2432]{2,1,0:T(2,128)(2,1)S(1)} async-done(((bf16[32,2,2432]{2,1,0:T(2,128)(2,1)}), bf16[32,2,2432]{2,1,0:T(2,128)(2,1)S(1)}, u32[]{:S(2)}, u32[]{:S(2)}) %all-to-all-start.1) | async-done | bytes 311328 | tf_op jit(solution)/shard_map/all_to_all | solution.py:11
  109.5 0.3 reshape.231
  109.8 0.3 reshape.209
  110.2 0.2 fusion.1
  110.5 0.2 fusion.17
  111.1 1.0 fusion.10
  112.1 2.1 %convolution_convert_fusion = bf16[192,1536]{1,0:T(8,128)(2,1)S(1)} fusion(bf16[1536,640]{1,0:T(8,128)(2,1)} %all-gather.2.cloned.1.call-done, bf16[96,512]{1,0:T(8,128)(2,1)S(1)} %bitcast.139, bf16[96,512]{1,0:T(8,128)(2,1)S(1)} %get-tuple-element.9), kind=kOutput, calls=%fused_computation | convolution fusion | flops 302678016 | bytes 2359296 | tf_op jit(solution)/shard_map/ot,it->oi/dot_general | solution.py:174
  114.2 1.1 convert_element_type.128
  115.3 6.8 %all-to-all-start.2 = ((bf16[32,6,1536]{2,1,0:T(8,128)(2,1)}), bf16[32,6,1536]{2,1,0:T(8,128)(2,1)S(1)}, u32[]{:S(2)}, u32[]{:S(2)}) async-start(bf16[32,6,1536]{2,1,0:T(8,128)(2,1)} %convert_element_type.128), calls=%async_computation.2 | async-start | bytes 1572864 | tf_op jit(solution)/shard_map/all_to_all | solution.py:11
  122.2 0.3 copy.117
  122.6 1.2 reshape.217
  123.8 16.9 %all-to-all-done.2 = bf16[32,6,1536]{2,1,0:T(8,128)(2,1)S(1)} async-done(((bf16[32,6,1536]{2,1,0:T(8,128)(2,1)}), bf16[32,6,1536]{2,1,0:T(8,128)(2,1)S(1)}, u32[]{:S(2)}, u32[]{:S(2)}) %all-to-all-start.2) | async-done | bytes 589856 | tf_op jit(solution)/shard_map/all_to_all | solution.py:11
  141.0 1.3 broadcast_in_dim.9
  142.3 8.3 %all-to-all-start.3 = ((f32[32,6,1536]{2,1,0:T(8,128)}), f32[32,6,1536]{2,1,0:T(8,128)S(1)}, u32[]{:S(2)}, u32[]{:S(2)}) async-start(f32[32,6,1536]{2,1,0:T(8,128)} %broadcast_in_dim.9), calls=%async_computation.3 | async-start | bytes 3145728 | tf_op jit(solution)/shard_map/all_to_all | solution.py:11
  151.0 0.9 fusion.42
  151.9 33.4 %reduce-scatter.2.cloned.1.call-done = f32[144,128]{1,0:T(8,128)} async-done(((f32[2304,128]{1,0:T(8,128)}), f32[144,128]{1,0:T(8,128)}) %reduce-scatter.2.cloned.1.call-update) | async-done | bytes 73744 | tf_op jit(solution)/shard_map/reduce_scatter | solution.py:192
  185.3 0.7 slice.150
  186.0 0.7 reshape.219
  186.7 0.8 slice.149
  187.5 0.6 reshape.218
  188.1 1.6 fusion.29
  189.9 0.9 slice.126
  190.8 0.9 slice.124
  (74 shorter events, 4.4 us)
Async XLA Ops:
  7.2 56.8 %copy-start = (bf16[96,1536]{1,0:T(8,128)(2,1)S(1)}, bf16[96,1536]{1,0:T(8,128)(2,1)}, u32[]{:S(2)}) copy-start(bf16[96,1536]{1,0:T(8,128)(2,1)} %param.10) | copy-start | bytes 884740
  7.2 54.1 %copy-start.1 = (bf16[2,256,256]{2,1,0:T(8,128)(2,1)S(1)}, bf16[2,256,256]{2,1,0:T(8,128)(2,1)}, u32[]{:S(2)}) copy-start(bf16[2,256,256]{2,1,0:T(8,128)(2,1)} %param.12) | copy-start | bytes 786436
  7.2 52.2 %all-gather.2.cloned.1.call-start = ((), (), s32[]{:S(2)}) async-start(), calls=%async_computation.5 | async-start | bytes 2088960 | tf_op jit(solution)/shard_map/all_gather | solution.py:51
  61.3 2.6 %copy-start.5 = (bf16[96,512]{1,0:T(8,128)(2,1)S(1)}, bf16[96,512]{1,0:T(8,128)(2,1)}, u32[]{:S(2)}) copy-start(bf16[96,512]{1,0:T(8,128)(2,1)} %param.17) | copy-start | bytes 294916
  66.7 11.7 %copy-start.4 = (s32[64]{0:T(128)S(1)}, s32[64]{0:T(128)}, u32[]{:S(2)}) copy-start(s32[64]{0:T(128)} %param.16) | copy-start | bytes 772
  69.1 19.4 %all-to-all-start = ((bf16[32,2,2176]{2,1,0:T(2,128)(2,1)}), bf16[32,2,2176]{2,1,0:T(2,128)(2,1)S(1)}, u32[]{:S(2)}, u32[]{:S(2)}) async-start(bf16[32,2,2176]{2,1,0:T(2,128)(2,1)} %reshape.228), calls=%async_computation | async-start | bytes 557056 | tf_op jit(solution)/shard_map/all_to_all | solution.py:11
  78.4 11.2 %copy-start.2 = (bf16[8,64,64]{2,1,0:T(8,128)(2,1)S(1)}, bf16[8,64,64]{2,1,0:T(8,128)(2,1)}, u32[]{:S(2)}) copy-start(bf16[8,64,64]{2,1,0:T(8,128)(2,1)} %param.13) | copy-start | bytes 196612
  89.4 1.5 copy-start.3
  92.8 16.7 %all-to-all-start.1 = ((bf16[32,2,2432]{2,1,0:T(2,128)(2,1)}), bf16[32,2,2432]{2,1,0:T(2,128)(2,1)S(1)}, u32[]{:S(2)}, u32[]{:S(2)}) async-start(bf16[32,2,2432]{2,1,0:T(2,128)(2,1)} %reshape.230), calls=%async_computation.1 | async-start | bytes 622592 | tf_op jit(solution)/shard_map/all_to_all | solution.py:11
  115.3 25.5 %all-to-all-start.2 = ((bf16[32,6,1536]{2,1,0:T(8,128)(2,1)}), bf16[32,6,1536]{2,1,0:T(8,128)(2,1)S(1)}, u32[]{:S(2)}, u32[]{:S(2)}) async-start(bf16[32,6,1536]{2,1,0:T(8,128)(2,1)} %convert_element_type.128), calls=%async_computation.2 | async-start | bytes 1572864 | tf_op jit(solution)/shard_map/all_to_all | solution.py:11
  122.1 63.3 %reduce-scatter.2.cloned.1.call-start = ((), (), s32[]{:S(2)}) async-start(), calls=%async_computation.6 | async-start | bytes 1253376 | tf_op jit(solution)/shard_map/reduce_scatter | solution.py:192
  142.3 47.5 %all-to-all-start.3 = ((f32[32,6,1536]{2,1,0:T(8,128)}), f32[32,6,1536]{2,1,0:T(8,128)S(1)}, u32[]{:S(2)}, u32[]{:S(2)}) async-start(f32[32,6,1536]{2,1,0:T(8,128)} %broadcast_in_dim.9), calls=%async_computation.3 | async-start | bytes 3145728 | tf_op jit(solution)/shard_map/all_to_all | solution.py:11
Sparse Core Ops, SparseCore 0:
  10.7 48.6 all-gather.1
  125.7 59.5 reduce-scatter.1

commit v5 on v4

--- a/solution.py
+++ b/solution.py
@@ -2,6 +2,8 @@
 import jax.numpy as jnp
 from jax import lax
 from jax.sharding import PartitionSpec as P
+from jax.experimental import pallas as pl
+from jax.experimental.pallas import tpu as pltpu
 
 
 HIGHEST = lax.Precision.HIGHEST
@@ -24,6 +26,58 @@
 def join_hi_lo(x):
     n = x.shape[-1] // 2
     return x[..., :n].astype(jnp.float32) + x[..., n:].astype(jnp.float32)
+
+
+def nt_dot(a, b, precision=None):
+    return lax.dot_general(
+        a, b, (((1,), (1,)), ((), ())), precision=precision, preferred_element_type=jnp.float32
+    )
+
+
+def stage1_kernel(x_ref, gw_ref, vw_ref, cot_ref, mem_ref, gate_ref, val_ref, dmix_ref, perdoc_ref, doclat_ref, mx_ref):
+    tok = gate_ref.shape[1]
+    xt = x_ref[:, :tok]
+    down = x_ref[:, tok:].astype(jnp.float32)
+    g = jnp.dot(gw_ref[...], xt, preferred_element_type=jnp.float32)
+    v = jnp.dot(vw_ref[...], xt, preferred_element_type=jnp.float32)
+    gate_ref[...] = g
+    val_ref[...] = v.astype(jnp.bfloat16)
+    sig = 1.0 / (1.0 + jnp.exp(-g))
+    dm = cot_ref[...].astype(jnp.float32) * (g * sig)
+    dmix_ref[...] = dm.astype(jnp.bfloat16)
+    mem = mem_ref[...]
+    perdoc_ref[...] = nt_dot(dm, mem, HIGHEST)
+    mx = nt_dot(mem.astype(jnp.bfloat16), xt)
+    mx_ref[...] = mx
+    doclat_ref[...] = jnp.dot(mx, down, precision=HIGHEST, preferred_element_type=jnp.float32)
+
+
+def stage1(gathered_all, gate_weight, value_weight, cotangent, member):
+    rows, tok = cotangent.shape
+    n_doc = member.shape[0]
+    d_all = gathered_all.shape[0]
+    lat = gathered_all.shape[1] - tok
+    f32, bf16 = jnp.float32, jnp.bfloat16
+    out_shape = (
+        jax.ShapeDtypeStruct((rows, tok), f32),
+        jax.ShapeDtypeStruct((rows, tok), bf16),
+        jax.ShapeDtypeStruct((rows, tok), bf16),
+        jax.ShapeDtypeStruct((rows, n_doc), f32),
+        jax.ShapeDtypeStruct((n_doc, lat), f32),
+        jax.ShapeDtypeStruct((n_doc, d_all), f32),
+    )
+    flops = 4 * rows * d_all * tok + 2 * n_doc * tok * d_all + 12 * rows * tok * n_doc + 12 * n_doc * d_all * lat
+    nbytes = 2 * (gathered_all.size + gate_weight.size + value_weight.size + cotangent.size) + 4 * member.size
+    nbytes += 8 * rows * tok + 4 * (rows * n_doc + n_doc * lat + n_doc * d_all)
+    vmem = pl.BlockSpec(memory_space=pltpu.VMEM)
+    return pl.pallas_call(
+        stage1_kernel,
+        out_shape=out_shape,
+        in_specs=[vmem] * 5,
+        out_specs=[vmem] * 6,
+        cost_estimate=pl.CostEstimate(flops=flops, bytes_accessed=nbytes, transcendentals=rows * tok),
+        compiler_params=pltpu.CompilerParams(vmem_limit_bytes=48 * 1024 * 1024),
+    )(gathered_all, gate_weight, value_weight, cotangent, member)
 
 
 def body(
@@ -50,7 +104,6 @@
     packed = jnp.concatenate([tokens, down_latent], axis=1)
     gathered_all = lax.all_gather(packed, "chan", axis=0, tiled=True)
     gathered = gathered_all[:, :tok_cols]
-    down_full = gathered_all[:, tok_cols:]
 
     doc_ends = jnp.cumsum(doc_lengths)
     doc_begins = doc_ends - doc_lengths
@@ -60,15 +113,11 @@
     ).astype(jnp.float32)
     len_scale = lax.rsqrt(doc_lengths.astype(jnp.float32))
 
-    gate_pre = jnp.dot(gate_weight, gathered, preferred_element_type=jnp.float32)
-    value_bf = jnp.dot(value_weight, gathered, preferred_element_type=jnp.float32).astype(
-        jnp.bfloat16
-    )
-    latent = jnp.einsum("ct,cl->lt", gathered, down_full, preferred_element_type=jnp.float32)
-    doc_lat_part = jnp.einsum("dt,lt->dl", member, latent, precision=HIGHEST)
-    xdoc_part = jnp.einsum(
-        "ct,dt->cd", tokens, member.astype(jnp.bfloat16), preferred_element_type=jnp.float32
-    )
+    gate_pre, value_bf, d_mixed_bf, per_doc_part, doc_lat_part, mx = stage1(
+        gathered_all, gate_weight, value_weight, cotangent, member
+    )
+    chan_me = lax.axis_index("chan")
+    xdoc_part = lax.dynamic_slice_in_dim(mx, chan_me * chan_rows, chan_rows, axis=1).T
 
     blocked = value_bf.reshape(chan_rows, blocks_here, block_width)
     inner_mix = jnp.einsum(
@@ -78,9 +127,6 @@
     sig = jax.nn.sigmoid(gate_pre)
     act = gate_pre * sig
     upstream = cotangent.astype(jnp.float32)
-    d_mixed = upstream * act
-    d_mixed_bf = d_mixed.astype(jnp.bfloat16)
-    per_doc_part = jnp.einsum("ct,dt->cd", d_mixed, member, precision=HIGHEST)
 
     inner_send = inner_mix.reshape(blocks_here, n_seq, k_here, chan_rows).transpose(1, 0, 2, 3)
     d_send = d_mixed_bf.reshape(chan_rows, blocks_here, n_seq, k_here).transpose(2, 1, 3, 0)

time: 201 us -> 207 us (1.030)
  local copies, waits for them, and re-layouts: 15.6 us -> 25.5 us
  matrix products: 14.5 us -> 8.23 us
    dot_general x6 -> x0, matrix products: 7.36 us -> none  [the longest x1 1.96 us: body(): jnp.einsum('ct,cl->lt', gathered, down_full, preferred_element_type=jnp.f...]
    unnamed x21 -> x41, local copies, waits for them, and re-layouts: 2.51 us -> 7.85 us
where the time goes in v5:
time: 207 us; the launch traced here: 204 us
  waiting for transfers between devices  117 us (57%)
  starting transfers between devices  31.5 us (15%)
  local copies, waits for them, and re-layouts  25.5 us (12%)
  between operations  14.6 us (7%)
  matrix products  8.23 us (4%)
  other arithmetic  5.76 us (3%)
    all_gather x1, waiting for transfers between devices, body(): gathered_all = lax.all_gather(packed, 'chan', axis=0, tiled=True)  48.2 us
    all_to_all x4, waiting for transfers between devices, seq_exchange(): return lax.all_to_all(x, 'seq', 0, 0, tiled=True)  35.4 us
    reduce_scatter x1, waiting for transfers between devices, body(): lax.psum_scatter(fac_send.reshape(-1, 128), 'chan', scatter_dimension=0,...  33.5 us
    all_to_all x4, starting transfers between devices, seq_exchange(): return lax.all_to_all(x, 'seq', 0, 0, tiled=True)  31.4 us
    unnamed x41, local copies, waits for them, and re-layouts  7.85 us
  transfers between devices with their start and end apart: 6, of which 5 were waited for; matrix products, arithmetic and copies ran while one was open for 6% of the time, Pallas kernels for 0%

profile of v5, /device:TPU:1, one launch (start us, length us, event | category | flops | bytes accessed | tf_op | source)
XLA Modules:
  0.0 204.1 jit_solution(17217714271985614462)
XLA Ops:
  7.2 1.6 pad_maximum_fusion.2
  8.9 0.7 copy.82
  9.8 0.7 sub.12
  10.5 0.6 copy-done.10
  11.2 48.2 %all-gather.2.cloned.1.call-done.x_ref = bf16[1536,640]{1,0:T(8,128)(2,1)} async-done(((bf16[96,640]{1,0:T(8,128)(2,1)}), bf16[1536,640]{1,0:T(8,128)(2,1)}) %all-gather.2.cloned.1.call-update) | async-done | bytes 1966096 | tf_op jit(solution)/shard_map/all_gather | solution.py:105
  59.4 1.5 copy-done.1
  60.9 1.0 copy-done.3
  61.9 1.0 copy-done.4
  62.9 0.9 copy-done.5
  63.7 1.6 shard_map.144
  66.9 0.5 broadcast.22
  67.5 0.8 reduce.1
  68.3 0.8 reshape.228
  69.0 9.3 %all-to-all-start = ((bf16[32,2,2176]{2,1,0:T(2,128)(2,1)}), bf16[32,2,2176]{2,1,0:T(2,128)(2,1)S(1)}, u32[]{:S(2)}, u32[]{:S(2)}) async-start(bf16[32,2,2176]{2,1,0:T(2,128)(2,1)} %reshape.228), calls=%async_computation | async-start | bytes 557056 | tf_op jit(solution)/shard_map/all_to_all | solution.py:13
  78.4 0.4 copy-done.14
  78.8 9.6 %all-to-all-done = bf16[32,2,2176]{2,1,0:T(2,128)(2,1)S(1)} async-done(((bf16[32,2,2176]{2,1,0:T(2,128)(2,1)}), bf16[32,2,2176]{2,1,0:T(2,128)(2,1)S(1)}, u32[]{:S(2)}, u32[]{:S(2)}) %all-to-all-start) | async-done | bytes 278560 | tf_op jit(solution)/shard_map/all_to_all | solution.py:13
  89.0 0.3 reshape.200
  90.6 0.3 reshape.205
  91.1 0.8 reduce.2
  92.0 0.8 reshape.230
  92.8 6.8 %all-to-all-start.1 = ((bf16[32,2,2432]{2,1,0:T(2,128)(2,1)}), bf16[32,2,2432]{2,1,0:T(2,128)(2,1)S(1)}, u32[]{:S(2)}, u32[]{:S(2)}) async-start(bf16[32,2,2432]{2,1,0:T(2,128)(2,1)} %reshape.230), calls=%async_computation.1 | async-start | bytes 622592 | tf_op jit(solution)/shard_map/all_to_all | solution.py:13
  99.8 0.9 reshape.216
  100.7 8.7 %all-to-all-done.1 = bf16[32,2,2432]{2,1,0:T(2,128)(2,1)S(1)} async-done(((bf16[32,2,2432]{2,1,0:T(2,128)(2,1)}), bf16[32,2,2432]{2,1,0:T(2,128)(2,1)S(1)}, u32[]{:S(2)}, u32[]{:S(2)}) %all-to-all-start.1) | async-done | bytes 311328 | tf_op jit(solution)/shard_map/all_to_all | solution.py:13
  109.4 0.3 reshape.231
  109.8 0.3 reshape.209
  110.1 0.8 slice_bitcast_fusion
  110.9 0.9 fusion.2
  112.2 1.1 copy.99
  113.3 0.8 copy.100
  114.1 0.9 copy.118
  115.0 2.0 multiply_convert_fusion
  117.0 1.5 convolution_convert_fusion
  118.4 2.1 %convert_element_type.112 = bf16[32,6,1536]{2,1,0:T(8,128)(2,1)} reshape(bf16[192,1536]{1,0:T(8,128)(2,1)} %convolution_convert_fusion) | data formatting | bytes 1179648 | tf_op jit(solution)/shard_map/convert_element_type | solution.py:224
  120.6 6.9 %all-to-all-start.2 = ((bf16[32,6,1536]{2,1,0:T(8,128)(2,1)}), bf16[32,6,1536]{2,1,0:T(8,128)(2,1)S(1)}, u32[]{:S(2)}, u32[]{:S(2)}) async-start(bf16[32,6,1536]{2,1,0:T(8,128)(2,1)} %convert_element_type.112), calls=%async_computation.2 | async-start | bytes 1572864 | tf_op jit(solution)/shard_map/all_to_all | solution.py:13
  127.6 0.3 copy.119
  128.0 1.2 reshape.217
  129.3 17.0 %all-to-all-done.2 = bf16[32,6,1536]{2,1,0:T(8,128)(2,1)S(1)} async-done(((bf16[32,6,1536]{2,1,0:T(8,128)(2,1)}), bf16[32,6,1536]{2,1,0:T(8,128)(2,1)S(1)}, u32[]{:S(2)}, u32[]{:S(2)}) %all-to-all-start.2) | async-done | bytes 589856 | tf_op jit(solution)/shard_map/all_to_all | solution.py:13
  146.4 1.3 broadcast_in_dim.9
  147.8 8.4 %all-to-all-start.3 = ((f32[32,6,1536]{2,1,0:T(8,128)}), f32[32,6,1536]{2,1,0:T(8,128)S(1)}, u32[]{:S(2)}, u32[]{:S(2)}) async-start(f32[32,6,1536]{2,1,0:T(8,128)} %broadcast_in_dim.9), calls=%async_computation.3 | async-start | bytes 3145728 | tf_op jit(solution)/shard_map/all_to_all | solution.py:13
  156.6 0.9 fusion.32
  157.5 33.5 %reduce-scatter.2.cloned.1.call-done = f32[144,128]{1,0:T(8,128)} async-done(((f32[2304,128]{1,0:T(8,128)}), f32[144,128]{1,0:T(8,128)}) %reduce-scatter.2.cloned.1.call-update) | async-done | bytes 73744 | tf_op jit(solution)/shard_map/reduce_scatter | solution.py:238
  191.0 0.7 slice.145
  191.7 0.7 reshape.219
  192.4 0.8 slice.144
  193.1 0.6 reshape.218
  193.8 1.6 fusion.21
  195.5 0.9 slice.122
  196.4 0.9 slice.120
  (92 shorter events, 5.6 us)
Async XLA Ops:
  7.2 58.7 %copy-start = (bf16[2,256,256]{2,1,0:T(8,128)(2,1)S(1)}, bf16[2,256,256]{2,1,0:T(8,128)(2,1)}, u32[]{:S(2)}) copy-start(bf16[2,256,256]{2,1,0:T(8,128)(2,1)} %param.12) | copy-start | bytes 786436
  7.2 52.2 %all-gather.2.cloned.1.call-start = ((), (), s32[]{:S(2)}) async-start(), calls=%async_computation.5 | async-start | bytes 2088960 | tf_op jit(solution)/shard_map/all_gather | solution.py:105
  9.8 1.3 copy-start.11
  10.5 0.7 copy-start.13
  10.5 0.6 copy-start.10
  59.4 1.5 copy-start.1
  60.9 1.0 copy-start.3
  61.9 1.0 copy-start.4
  62.8 0.9 copy-start.5
  66.5 11.8 %copy-start.12 = (s32[64]{0:T(128)S(1)}, s32[64]{0:T(128)}, u32[]{:S(2)}) copy-start(s32[64]{0:T(128)} %param.16) | copy-start | bytes 772
  69.0 19.4 %all-to-all-start = ((bf16[32,2,2176]{2,1,0:T(2,128)(2,1)}), bf16[32,2,2176]{2,1,0:T(2,128)(2,1)S(1)}, u32[]{:S(2)}, u32[]{:S(2)}) async-start(bf16[32,2,2176]{2,1,0:T(2,128)(2,1)} %reshape.228), calls=%async_computation | async-start | bytes 557056 | tf_op jit(solution)/shard_map/all_to_all | solution.py:13
  78.3 0.5 copy-start.14
  78.8 10.8 %copy-start.7 = (bf16[8,64,64]{2,1,0:T(8,128)(2,1)S(1)}, bf16[8,64,64]{2,1,0:T(8,128)(2,1)}, u32[]{:S(2)}) copy-start(bf16[8,64,64]{2,1,0:T(8,128)(2,1)} %param.13) | copy-start | bytes 196612
  89.3 1.5 copy-start.9
  92.8 16.7 %all-to-all-start.1 = ((bf16[32,2,2432]{2,1,0:T(2,128)(2,1)}), bf16[32,2,2432]{2,1,0:T(2,128)(2,1)S(1)}, u32[]{:S(2)}, u32[]{:S(2)}) async-start(bf16[32,2,2432]{2,1,0:T(2,128)(2,1)} %reshape.230), calls=%async_computation.1 | async-start | bytes 622592 | tf_op jit(solution)/shard_map/all_to_all | solution.py:13
  110.1 4.9 %copy-start.6 = (bf16[96,512]{1,0:T(8,128)(2,1)S(1)}, bf16[96,512]{1,0:T(8,128)(2,1)}, u32[]{:S(2)}) copy-start(bf16[96,512]{1,0:T(8,128)(2,1)} %cot_ref.1) | copy-start | bytes 294916
  111.9 5.0 %copy-start.2 = (bf16[1536,640]{1,0:T(8,128)(2,1)S(1)}, bf16[1536,640]{1,0:T(8,128)(2,1)}, u32[]{:S(2)}) copy-start(bf16[1536,640]{1,0:T(8,128)(2,1)} %all-gather.2.cloned.1.call-done.x_ref) | copy-start | bytes 5898244
  120.6 7.4 %copy-start.8 = (f32[16,2048]{1,0:T(8,128)S(1)}, f32[16,2048]{1,0:T(8,128)}, u32[]{:S(2)}) copy-start(f32[16,2048]{1,0:T(8,128)} %reshape.216) | copy-start | bytes 393220
  120.6 25.7 %all-to-all-start.2 = ((bf16[32,6,1536]{2,1,0:T(8,128)(2,1)}), bf16[32,6,1536]{2,1,0:T(8,128)(2,1)S(1)}, u32[]{:S(2)}, u32[]{:S(2)}) async-start(bf16[32,6,1536]{2,1,0:T(8,128)(2,1)} %convert_element_type.112), calls=%async_computation.2 | async-start | bytes 1572864 | tf_op jit(solution)/shard_map/all_to_all | solution.py:13
  127.5 63.5 %reduce-scatter.2.cloned.1.call-start = ((), (), s32[]{:S(2)}) async-start(), calls=%async_computation.6 | async-start | bytes 1253376 | tf_op jit(solution)/shard_map/reduce_scatter | solution.py:238
  147.8 46.0 %copy-start.15 = (f32[64]{0:T(128)S(1)}, f32[64]{0:T(128)}, u32[]{:S(2)}) copy-start(f32[64]{0:T(128)} %copy-done.14) | copy-start | bytes 772
  147.8 47.6 %all-to-all-start.3 = ((f32[32,6,1536]{2,1,0:T(8,128)}), f32[32,6,1536]{2,1,0:T(8,128)S(1)}, u32[]{:S(2)}, u32[]{:S(2)}) async-start(f32[32,6,1536]{2,1,0:T(8,128)} %broadcast_in_dim.9), calls=%async_computation.3 | async-start | bytes 3145728 | tf_op jit(solution)/shard_map/all_to_all | solution.py:13
Sparse Core Ops, SparseCore 0:
  10.7 48.6 all-gather.1
  131.2 59.7 reduce-scatter.1

commit v6 on v5

--- a/solution.py
+++ b/solution.py
@@ -34,21 +34,43 @@
     )
 
 
-def stage1_kernel(x_ref, gw_ref, vw_ref, cot_ref, mem_ref, gate_ref, val_ref, dmix_ref, perdoc_ref, doclat_ref, mx_ref):
+def stage1_kernel(
+    x_hbm, gw_hbm, vw_hbm, cot_hbm, mem_hbm,
+    gate_ref, val_ref, dmix_ref, perdoc_ref, doclat_ref, mx_ref,
+    x_v, gw_v, vw_v, cot_v, mem_v, sems,
+):
     tok = gate_ref.shape[1]
-    xt = x_ref[:, :tok]
-    down = x_ref[:, tok:].astype(jnp.float32)
-    g = jnp.dot(gw_ref[...], xt, preferred_element_type=jnp.float32)
-    v = jnp.dot(vw_ref[...], xt, preferred_element_type=jnp.float32)
+    half = x_v.shape[0] // 2
+    copies = [
+        pltpu.make_async_copy(gw_hbm, gw_v, sems.at[0]),
+        pltpu.make_async_copy(x_hbm.at[pl.ds(0, half)], x_v.at[pl.ds(0, half)], sems.at[1]),
+        pltpu.make_async_copy(x_hbm.at[pl.ds(half, half)], x_v.at[pl.ds(half, half)], sems.at[2]),
+        pltpu.make_async_copy(vw_hbm, vw_v, sems.at[3]),
+        pltpu.make_async_copy(cot_hbm, cot_v, sems.at[4]),
+        pltpu.make_async_copy(mem_hbm, mem_v, sems.at[5]),
+    ]
+    for c in copies:
+        c.start()
+    copies[0].wait()
+    copies[1].wait()
+    g = jnp.dot(gw_v[:, :half], x_v[:half, :tok], preferred_element_type=jnp.float32)
+    copies[2].wait()
+    g = g + jnp.dot(gw_v[:, half:], x_v[half:, :tok], preferred_element_type=jnp.float32)
     gate_ref[...] = g
+    copies[3].wait()
+    xt = x_v[:, :tok]
+    v = jnp.dot(vw_v[...], xt, preferred_element_type=jnp.float32)
     val_ref[...] = v.astype(jnp.bfloat16)
     sig = 1.0 / (1.0 + jnp.exp(-g))
-    dm = cot_ref[...].astype(jnp.float32) * (g * sig)
+    copies[4].wait()
+    dm = cot_v[...].astype(jnp.float32) * (g * sig)
     dmix_ref[...] = dm.astype(jnp.bfloat16)
-    mem = mem_ref[...]
+    copies[5].wait()
+    mem = mem_v[...]
     perdoc_ref[...] = nt_dot(dm, mem, HIGHEST)
     mx = nt_dot(mem.astype(jnp.bfloat16), xt)
     mx_ref[...] = mx
+    down = x_v[:, tok:].astype(jnp.float32)
     doclat_ref[...] = jnp.dot(mx, down, precision=HIGHEST, preferred_element_type=jnp.float32)
 
 
@@ -69,15 +91,16 @@
     flops = 4 * rows * d_all * tok + 2 * n_doc * tok * d_all + 12 * rows * tok * n_doc + 12 * n_doc * d_all * lat
     nbytes = 2 * (gathered_all.size + gate_weight.size + value_weight.size + cotangent.size) + 4 * member.size
     nbytes += 8 * rows * tok + 4 * (rows * n_doc + n_doc * lat + n_doc * d_all)
-    vmem = pl.BlockSpec(memory_space=pltpu.VMEM)
+    operands = (gathered_all, gate_weight, value_weight, cotangent, member)
     return pl.pallas_call(
         stage1_kernel,
         out_shape=out_shape,
-        in_specs=[vmem] * 5,
-        out_specs=[vmem] * 6,
+        in_specs=[pl.BlockSpec(memory_space=pl.ANY)] * 5,
+        out_specs=[pl.BlockSpec(memory_space=pltpu.VMEM)] * 6,
+        scratch_shapes=[pltpu.VMEM(a.shape, a.dtype) for a in operands]
+        + [pltpu.SemaphoreType.DMA((6,))],
         cost_estimate=pl.CostEstimate(flops=flops, bytes_accessed=nbytes, transcendentals=rows * tok),
-        compiler_params=pltpu.CompilerParams(vmem_limit_bytes=48 * 1024 * 1024),
-    )(gathered_all, gate_weight, value_weight, cotangent, member)
+    )(*operands)
 
 
 def body(

time: 207 us -> 205 us (level)
  local copies, waits for them, and re-layouts: 25.5 us -> 21.1 us
  Pallas kernels: 1.58 us -> 4.16 us
    unnamed x41 -> x37, local copies, waits for them, and re-layouts: 7.85 us -> 3.81 us
    pallas_call x1, Pallas kernels: 1.58 us -> 4.16 us  [stage1(): pl.pallas_call(stage1_kernel, out_shape=out_shape, in_specs=[pl.BlockSpec...]
  transfers between devices with their start and end apart: 6 -> 6, of which waited for: 5 -> 5; matrix products, arithmetic and copies ran while one was open for 6% -> 7% of each run, Pallas kernels for 0% -> 0%
where the time goes in v6:
time: 205 us; the launch traced here: 201 us
  waiting for transfers between devices  115 us (56%)
  starting transfers between devices  31.5 us (15%)
  local copies, waits for them, and re-layouts  21.1 us (10%)
  between operations  14.6 us (7%)
  matrix products  7.7 us (4%)
  other arithmetic  7.02 us (3%)
  Pallas kernels  4.16 us (2%)
    all_gather x1, waiting for transfers between devices, body(): gathered_all = lax.all_gather(packed, 'chan', axis=0, tiled=True)  46.9 us
    all_to_all x4, waiting for transfers between devices, seq_exchange(): return lax.all_to_all(x, 'seq', 0, 0, tiled=True)  35.2 us
    reduce_scatter x1, waiting for transfers between devices, body(): lax.psum_scatter(fac_send.reshape(-1, 128), 'chan', scatter_dimension=0,...  33.2 us
    all_to_all x4, starting transfers between devices, seq_exchange(): return lax.all_to_all(x, 'seq', 0, 0, tiled=True)  31.4 us
    pallas_call x1, Pallas kernels, stage1(): pl.pallas_call(stage1_kernel, out_shape=out_shape, in_specs=[pl.BlockSpec...  4.16 us
  transfers between devices with their start and end apart: 6, of which 5 were waited for; matrix products, arithmetic and copies ran while one was open for 7% of the time, Pallas kernels for 0%

profile of v6, /device:TPU:1, one launch (start us, length us, event | category | flops | bytes accessed | tf_op | source)
XLA Modules:
  0.0 201.4 jit_solution(5459216494243334088)
XLA Ops:
  7.2 1.6 pad_maximum_fusion.2
  8.9 0.7 copy.82
  9.8 0.7 sub.12
  10.5 0.6 iota_add_fusion
  11.1 1.4 fusion.11.mem_hbm
  12.5 46.9 %all-gather.2.cloned.1.call-done.x_hbm = bf16[1536,640]{1,0:T(8,128)(2,1)} async-done(((bf16[96,640]{1,0:T(8,128)(2,1)}), bf16[1536,640]{1,0:T(8,128)(2,1)}) %all-gather.2.cloned.1.call-update) | async-done | bytes 1966096 | tf_op jit(solution)/shard_map/all_gather | solution.py:128
  59.4 4.2 %shard_map.144 = (f32[96,512]{1,0:T(8,128)}, bf16[96,512]{1,0:T(8,128)(2,1)}, bf16[96,512]{1,0:T(8,128)(2,1)}, f32[96,64]{1,0:T(8,128)}, f32[64,128]{1,0:T(8,128)}, /*index=5*/f32[64,1536]{1,0:T(8,128)}) custom-call(bf16[1536,640]{1,0:T(8,128)(2,1)} %all-gather.2.cloned.1.call-done.x_hbm, bf16[96,1536]{1,0:T(8,128)(2,1)} %gw_hbm.1, bf16[96,1536]{1,0:T(8,128)(2,1)} %vw_hbm.1, ...), custom_call_target="tpu_custom_call" | custom-call | flops 591396864 | bytes 3629056 | tf_op jit(solution)/shard_map/pallas_call | solution.py:95
  63.6 0.8 reshape.195
  64.3 0.9 copy.87
  65.4 0.9 constant_dynamic-slice_fusion
  66.5 1.1 fusion.1
  67.8 1.0 copy.85
  69.0 0.3 reshape.194
  69.4 0.5 broadcast.22
  69.9 0.8 reduce.1
  70.7 0.8 reshape.228
  71.5 9.3 %all-to-all-start = ((bf16[32,2,2176]{2,1,0:T(2,128)(2,1)}), bf16[32,2,2176]{2,1,0:T(2,128)(2,1)S(1)}, u32[]{:S(2)}, u32[]{:S(2)}) async-start(bf16[32,2,2176]{2,1,0:T(2,128)(2,1)} %reshape.228), calls=%async_computation | async-start | bytes 557056 | tf_op jit(solution)/shard_map/all_to_all | solution.py:13
  80.8 0.5 copy-done.12
  81.3 9.5 %all-to-all-done = bf16[32,2,2176]{2,1,0:T(2,128)(2,1)S(1)} async-done(((bf16[32,2,2176]{2,1,0:T(2,128)(2,1)}), bf16[32,2,2176]{2,1,0:T(2,128)(2,1)S(1)}, u32[]{:S(2)}, u32[]{:S(2)}) %all-to-all-start) | async-done | bytes 278560 | tf_op jit(solution)/shard_map/all_to_all | solution.py:13
  90.9 0.2 reshape.229
  91.4 0.3 reshape.200
  93.0 0.2 reshape.205
  93.5 0.8 reduce.2
  94.4 0.8 reshape.230
  95.2 6.8 %all-to-all-start.1 = ((bf16[32,2,2432]{2,1,0:T(2,128)(2,1)}), bf16[32,2,2432]{2,1,0:T(2,128)(2,1)S(1)}, u32[]{:S(2)}, u32[]{:S(2)}) async-start(bf16[32,2,2432]{2,1,0:T(2,128)(2,1)} %reshape.230), calls=%async_computation.1 | async-start | bytes 622592 | tf_op jit(solution)/shard_map/all_to_all | solution.py:13
  102.2 0.9 reshape.216
  103.1 8.7 %all-to-all-done.1 = bf16[32,2,2432]{2,1,0:T(2,128)(2,1)S(1)} async-done(((bf16[32,2,2432]{2,1,0:T(2,128)(2,1)}), bf16[32,2,2432]{2,1,0:T(2,128)(2,1)S(1)}, u32[]{:S(2)}, u32[]{:S(2)}) %all-to-all-start.1) | async-done | bytes 311328 | tf_op jit(solution)/shard_map/all_to_all | solution.py:13
  111.8 0.3 reshape.231
  112.2 0.3 reshape.209
  113.2 0.6 copy.120
  114.2 2.0 %multiply_convert_fusion = (bf16[96,512]{1,0:T(8,128)(2,1)S(1)}, bf16[96,512]{1,0:T(8,128)(2,1)}) fusion(f32[96,512]{1,0:T(8,128)} %get-tuple-element.13, bf16[96,512]{1,0:T(8,128)(2,1)} %cot_hbm.1, f32[96,512]{1,0:T(8,128)S(1)} %copy.100, f32[64,96]{1,0:T(8,128)S(1)} %fusion.30, s32[512]{0:T(512)} %iota_add_fusion, s32[64]{0:T(128)} %copy-done.9, ...), kind=kOutput, calls=%fused_computation.23 | convolution fusion | flops 38584320 | bytes 715264 | tf_op jit(solution)/shard_map/dot_general | solution.py:229
  116.3 0.7 convolution_convert_fusion
  116.9 1.1 convert_element_type.112
  118.0 6.9 %all-to-all-start.2 = ((bf16[32,6,1536]{2,1,0:T(8,128)(2,1)}), bf16[32,6,1536]{2,1,0:T(8,128)(2,1)S(1)}, u32[]{:S(2)}, u32[]{:S(2)}) async-start(bf16[32,6,1536]{2,1,0:T(8,128)(2,1)} %convert_element_type.112), calls=%async_computation.2 | async-start | bytes 1572864 | tf_op jit(solution)/shard_map/all_to_all | solution.py:13
  125.1 0.3 copy.119
  125.5 1.2 reshape.217
  126.8 16.9 %all-to-all-done.2 = bf16[32,6,1536]{2,1,0:T(8,128)(2,1)S(1)} async-done(((bf16[32,6,1536]{2,1,0:T(8,128)(2,1)}), bf16[32,6,1536]{2,1,0:T(8,128)(2,1)S(1)}, u32[]{:S(2)}, u32[]{:S(2)}) %all-to-all-start.2) | async-done | bytes 589856 | tf_op jit(solution)/shard_map/all_to_all | solution.py:13
  143.9 1.4 broadcast_in_dim.9
  145.2 8.4 %all-to-all-start.3 = ((f32[32,6,1536]{2,1,0:T(8,128)}), f32[32,6,1536]{2,1,0:T(8,128)S(1)}, u32[]{:S(2)}, u32[]{:S(2)}) async-start(f32[32,6,1536]{2,1,0:T(8,128)} %broadcast_in_dim.9), calls=%async_computation.3 | async-start | bytes 3145728 | tf_op jit(solution)/shard_map/all_to_all | solution.py:13
  154.1 0.9 fusion.32
  155.0 33.2 %reduce-scatter.2.cloned.1.call-done = f32[144,128]{1,0:T(8,128)} async-done(((f32[2304,128]{1,0:T(8,128)}), f32[144,128]{1,0:T(8,128)}) %reduce-scatter.2.cloned.1.call-update) | async-done | bytes 73744 | tf_op jit(solution)/shard_map/reduce_scatter | solution.py:261
  188.2 0.7 slice.145
  188.9 0.7 reshape.219
  189.6 0.8 slice.144
  190.4 0.6 reshape.218
  191.0 1.6 fusion.21
  192.7 0.9 slice.122
  193.6 0.9 slice.120
  (88 shorter events, 5.1 us)
Async XLA Ops:
  7.2 59.4 %copy-start = (bf16[2,256,256]{2,1,0:T(8,128)(2,1)S(1)}, bf16[2,256,256]{2,1,0:T(8,128)(2,1)}, u32[]{:S(2)}) copy-start(bf16[2,256,256]{2,1,0:T(8,128)(2,1)} %param.12) | copy-start | bytes 786436
  7.2 52.2 %all-gather.2.cloned.1.call-start = ((), (), s32[]{:S(2)}) async-start(), calls=%async_computation.5 | async-start | bytes 2088960 | tf_op jit(solution)/shard_map/all_gather | solution.py:128
  9.8 54.5 %copy-start.9 = (s32[64]{0:T(128)}, s32[64]{0:T(128)S(1)}, u32[]{:S(2)}) copy-start(s32[64]{0:T(128)S(1)} %reduce) | copy-start | bytes 772
  10.5 53.1 %copy-start.11 = (s32[64]{0:T(128)}, s32[64]{0:T(128)S(1)}, u32[]{:S(2)}) copy-start(s32[64]{0:T(128)S(1)} %sub.12) | copy-start | bytes 772
  68.9 11.8 %copy-start.10 = (s32[64]{0:T(128)S(1)}, s32[64]{0:T(128)}, u32[]{:S(2)}) copy-start(s32[64]{0:T(128)} %param.16) | copy-start | bytes 772
  71.5 19.4 %all-to-all-start = ((bf16[32,2,2176]{2,1,0:T(2,128)(2,1)}), bf16[32,2,2176]{2,1,0:T(2,128)(2,1)S(1)}, u32[]{:S(2)}, u32[]{:S(2)}) async-start(bf16[32,2,2176]{2,1,0:T(2,128)(2,1)} %reshape.228), calls=%async_computation | async-start | bytes 557056 | tf_op jit(solution)/shard_map/all_to_all | solution.py:13
  80.7 0.6 copy-start.12
  81.3 10.7 %copy-start.2 = (bf16[8,64,64]{2,1,0:T(8,128)(2,1)S(1)}, bf16[8,64,64]{2,1,0:T(8,128)(2,1)}, u32[]{:S(2)}) copy-start(bf16[8,64,64]{2,1,0:T(8,128)(2,1)} %param.13) | copy-start | bytes 196612
  91.7 1.5 copy-start.8
  95.2 16.7 %all-to-all-start.1 = ((bf16[32,2,2432]{2,1,0:T(2,128)(2,1)}), bf16[32,2,2432]{2,1,0:T(2,128)(2,1)S(1)}, u32[]{:S(2)}, u32[]{:S(2)}) async-start(bf16[32,2,2432]{2,1,0:T(2,128)(2,1)} %reshape.230), calls=%async_computation.1 | async-start | bytes 622592 | tf_op jit(solution)/shard_map/all_to_all | solution.py:13
  112.1 0.9 copy-start.4
  113.2 3.1 %copy-start.1 = (bf16[1536,640]{1,0:T(8,128)(2,1)S(1)}, bf16[1536,640]{1,0:T(8,128)(2,1)}, u32[]{:S(2)}) copy-start(bf16[1536,640]{1,0:T(8,128)(2,1)} %all-gather.2.cloned.1.call-done.x_hbm) | copy-start | bytes 5898244
  113.9 2.4 %copy-start.5 = (f32[64,128]{1,0:T(8,128)}, f32[64,128]{1,0:T(8,128)S(1)}, u32[]{:S(2)}) copy-start(f32[64,128]{1,0:T(8,128)S(1)} %reshape.210) | copy-start | bytes 98308
  118.0 7.4 %copy-start.7 = (f32[4,2,8,128]{3,1,2,0:T(2,128)S(1)}, f32[4,2,8,128]{3,1,2,0:T(2,128)}, u32[]{:S(2)}) copy-start(f32[4,2,8,128]{3,1,2,0:T(2,128)} %copy.120) | copy-start | bytes 98308
  118.0 7.4 %copy-start.3 = (f32[16,2048]{1,0:T(8,128)S(1)}, f32[16,2048]{1,0:T(8,128)}, u32[]{:S(2)}) copy-start(f32[16,2048]{1,0:T(8,128)} %reshape.216) | copy-start | bytes 393220
  118.0 25.7 %all-to-all-start.2 = ((bf16[32,6,1536]{2,1,0:T(8,128)(2,1)}), bf16[32,6,1536]{2,1,0:T(8,128)(2,1)S(1)}, u32[]{:S(2)}, u32[]{:S(2)}) async-start(bf16[32,6,1536]{2,1,0:T(8,128)(2,1)} %convert_element_type.112), calls=%async_computation.2 | async-start | bytes 1572864 | tf_op jit(solution)/shard_map/all_to_all | solution.py:13
  125.0 63.2 %reduce-scatter.2.cloned.1.call-start = ((), (), s32[]{:S(2)}) async-start(), calls=%async_computation.6 | async-start | bytes 1253376 | tf_op jit(solution)/shard_map/reduce_scatter | solution.py:261
  145.2 8.9 %copy-start.6 = (f32[64,128]{1,0:T(8,128)S(1)}, f32[64,128]{1,0:T(8,128)}, u32[]{:S(2)}) copy-start(f32[64,128]{1,0:T(8,128)} %copy-done.5) | copy-start | bytes 98308
  145.2 45.8 %copy-start.13 = (f32[64]{0:T(128)S(1)}, f32[64]{0:T(128)}, u32[]{:S(2)}) copy-start(f32[64]{0:T(128)} %copy-done.12) | copy-start | bytes 772
  145.2 47.4 %all-to-all-start.3 = ((f32[32,6,1536]{2,1,0:T(8,128)}), f32[32,6,1536]{2,1,0:T(8,128)S(1)}, u32[]{:S(2)}, u32[]{:S(2)}) async-start(f32[32,6,1536]{2,1,0:T(8,128)} %broadcast_in_dim.9), calls=%async_computation.3 | async-start | bytes 3145728 | tf_op jit(solution)/shard_map/all_to_all | solution.py:13
Sparse Core Ops, SparseCore 0:
  10.7 48.6 all-gather.1
  128.6 59.5 reduce-scatter.1

commit v7 on v4

--- a/solution.py
+++ b/solution.py
@@ -9,10 +9,6 @@
 
 def seq_exchange(x):
     return lax.all_to_all(x, "seq", 0, 0, tiled=True)
-
-
-def chan_exchange(x):
-    return lax.all_to_all(x, "chan", 0, 0, tiled=True)
 
 
 def split_hi_lo(x):
@@ -189,9 +185,8 @@
     )
     g_send = jnp.broadcast_to(g_gath, (n_chan, n_doc * lat))
     fac_send = jnp.concatenate([first_send, second_send, g_send], axis=1)
-    fac_red = lax.psum_scatter(
-        fac_send.reshape(-1, 128), "chan", scatter_dimension=0, tiled=True
-    ).reshape(-1)
+    fac_red = lax.psum_scatter(fac_send.reshape(-1, 128), "chan", scatter_dimension=0, tiled=True)
+    fac_red = fac_red.reshape(-1)
     n_f = blocks_here * k_part * block_width
     d_first = fac_red[:n_f].reshape(blocks_here, k_part, block_width)
     n_s = k_here * m_part * n_blk2
@@ -228,4 +223,5 @@
         P("chan", None),
         P("chan", None),
     )
+
     return jax.shard_map(body, mesh=mesh, in_specs=in_specs, out_specs=out_specs, check_vma=False)

time: 201 us -> 201 us (level)
  no operation moved by 1% of the time
where the time goes in v7:
time: 201 us; the launch traced here: 198 us
  waiting for transfers between devices  117 us (58%)
  starting transfers between devices  31.2 us (16%)
  local copies, waits for them, and re-layouts  15.6 us (8%)
  between operations  14.6 us (7%)
  matrix products  14.5 us (7%)
  other arithmetic  5.08 us (3%)
    all_gather x1, waiting for transfers between devices, body(): gathered_all = lax.all_gather(packed, 'chan', axis=0, tiled=True)  47.6 us
    all_to_all x4, waiting for transfers between devices, seq_exchange(): return lax.all_to_all(x, 'seq', 0, 0, tiled=True)  36.4 us
    reduce_scatter x1, waiting for transfers between devices, body(): lax.psum_scatter(fac_send.reshape(-1, 128), 'chan', scatter_dimension=0,...  33.4 us
    all_to_all x4, starting transfers between devices, seq_exchange(): return lax.all_to_all(x, 'seq', 0, 0, tiled=True)  31.1 us
  transfers between devices with their start and end apart: 6, of which 5 were waited for; matrix products, arithmetic and copies ran while one was open for 6% of the time, Pallas kernels for 0%

profile of v7, /device:TPU:1, one launch (start us, length us, event | category | flops | bytes accessed | tf_op | source)
XLA Modules:
  0.0 198.5 jit_solution(10429211262752419553)
XLA Ops:
  7.2 1.6 pad_maximum_fusion.2
  8.9 0.7 copy.85
  9.9 0.7 sub.12
  10.5 1.1 fusion.27
  11.8 47.6 %all-gather.2.cloned.1.call-done = bf16[1536,640]{1,0:T(8,128)(2,1)} async-done(((bf16[96,640]{1,0:T(8,128)(2,1)}), bf16[1536,640]{1,0:T(8,128)(2,1)}) %all-gather.2.cloned.1.call-update) | async-done | bytes 1966096 | tf_op jit(solution)/shard_map/all_gather | solution.py:47
  59.4 1.9 convolution_convert_fusion.3
  61.3 0.2 fusion
  61.7 2.0 fusion.3
  63.6 0.3 fusion.35
  63.9 1.8 fusion.16
  66.1 0.2 reshape.192
  66.3 0.3 fusion.15
  67.0 0.5 broadcast.29
  67.5 0.8 reduce.1
  68.3 0.8 reshape.228
  69.1 9.3 %all-to-all-start = ((bf16[32,2,2176]{2,1,0:T(2,128)(2,1)}), bf16[32,2,2176]{2,1,0:T(2,128)(2,1)S(1)}, u32[]{:S(2)}, u32[]{:S(2)}) async-start(bf16[32,2,2176]{2,1,0:T(2,128)(2,1)} %reshape.228), calls=%async_computation | async-start | bytes 557056 | tf_op jit(solution)/shard_map/all_to_all | solution.py:11
  78.4 10.1 %all-to-all-done = bf16[32,2,2176]{2,1,0:T(2,128)(2,1)S(1)} async-done(((bf16[32,2,2176]{2,1,0:T(2,128)(2,1)}), bf16[32,2,2176]{2,1,0:T(2,128)(2,1)S(1)}, u32[]{:S(2)}, u32[]{:S(2)}) %all-to-all-start) | async-done | bytes 278560 | tf_op jit(solution)/shard_map/all_to_all | solution.py:11
  88.5 0.2 reshape.229
  89.1 0.3 reshape.200
  90.1 0.2 convolution_convert_fusion.2
  90.6 0.3 reshape.205
  91.2 0.8 reduce.2
  92.0 0.8 reshape.230
  92.8 6.8 %all-to-all-start.1 = ((bf16[32,2,2432]{2,1,0:T(2,128)(2,1)}), bf16[32,2,2432]{2,1,0:T(2,128)(2,1)S(1)}, u32[]{:S(2)}, u32[]{:S(2)}) async-start(bf16[32,2,2432]{2,1,0:T(2,128)(2,1)} %reshape.230), calls=%async_computation.1 | async-start | bytes 622592 | tf_op jit(solution)/shard_map/all_to_all | solution.py:11
  99.8 0.2 reshape.216
  100.1 9.4 %all-to-all-done.1 = bf16[32,2,2432]{2,1,0:T(2,128)(2,1)S(1)} async-done(((bf16[32,2,2432]{2,1,0:T(2,128)(2,1)}), bf16[32,2,2432]{2,1,0:T(2,128)(2,1)S(1)}, u32[]{:S(2)}, u32[]{:S(2)}) %all-to-all-start.1) | async-done | bytes 311328 | tf_op jit(solution)/shard_map/all_to_all | solution.py:11
  109.5 0.3 reshape.231
  109.8 0.3 reshape.209
  110.2 0.2 fusion.1
  110.5 0.2 fusion.17
  111.1 1.0 fusion.10
  112.1 2.1 %convolution_convert_fusion = bf16[192,1536]{1,0:T(8,128)(2,1)S(1)} fusion(bf16[1536,640]{1,0:T(8,128)(2,1)} %all-gather.2.cloned.1.call-done, bf16[96,512]{1,0:T(8,128)(2,1)S(1)} %bitcast.139, bf16[96,512]{1,0:T(8,128)(2,1)S(1)} %get-tuple-element.9), kind=kOutput, calls=%fused_computation | convolution fusion | flops 302678016 | bytes 2359296 | tf_op jit(solution)/shard_map/ot,it->oi/dot_general | solution.py:170
  114.2 1.1 convert_element_type.128
  115.3 6.8 %all-to-all-start.2 = ((bf16[32,6,1536]{2,1,0:T(8,128)(2,1)}), bf16[32,6,1536]{2,1,0:T(8,128)(2,1)S(1)}, u32[]{:S(2)}, u32[]{:S(2)}) async-start(bf16[32,6,1536]{2,1,0:T(8,128)(2,1)} %convert_element_type.128), calls=%async_computation.2 | async-start | bytes 1572864 | tf_op jit(solution)/shard_map/all_to_all | solution.py:11
  122.2 0.3 copy.117
  122.6 1.2 reshape.217
  123.8 16.9 %all-to-all-done.2 = bf16[32,6,1536]{2,1,0:T(8,128)(2,1)S(1)} async-done(((bf16[32,6,1536]{2,1,0:T(8,128)(2,1)}), bf16[32,6,1536]{2,1,0:T(8,128)(2,1)S(1)}, u32[]{:S(2)}, u32[]{:S(2)}) %all-to-all-start.2) | async-done | bytes 589856 | tf_op jit(solution)/shard_map/all_to_all | solution.py:11
  141.0 1.3 broadcast_in_dim.9
  142.3 8.3 %all-to-all-start.3 = ((f32[32,6,1536]{2,1,0:T(8,128)}), f32[32,6,1536]{2,1,0:T(8,128)S(1)}, u32[]{:S(2)}, u32[]{:S(2)}) async-start(f32[32,6,1536]{2,1,0:T(8,128)} %broadcast_in_dim.9), calls=%async_computation.3 | async-start | bytes 3145728 | tf_op jit(solution)/shard_map/all_to_all | solution.py:11
  151.0 0.9 fusion.42
  151.9 33.4 %reduce-scatter.2.cloned.1.call-done = f32[144,128]{1,0:T(8,128)} async-done(((f32[2304,128]{1,0:T(8,128)}), f32[144,128]{1,0:T(8,128)}) %reduce-scatter.2.cloned.1.call-update) | async-done | bytes 73744 | tf_op jit(solution)/shard_map/reduce_scatter | solution.py:188
  185.3 0.7 slice.150
  186.0 0.7 reshape.219
  186.7 0.8 slice.149
  187.5 0.6 reshape.218
  188.1 1.6 fusion.29
  189.9 0.9 slice.126
  190.8 0.9 slice.124
  (74 shorter events, 4.4 us)
Async XLA Ops:
  7.2 56.8 %copy-start = (bf16[96,1536]{1,0:T(8,128)(2,1)S(1)}, bf16[96,1536]{1,0:T(8,128)(2,1)}, u32[]{:S(2)}) copy-start(bf16[96,1536]{1,0:T(8,128)(2,1)} %param.10) | copy-start | bytes 884740
  7.2 54.1 %copy-start.1 = (bf16[2,256,256]{2,1,0:T(8,128)(2,1)S(1)}, bf16[2,256,256]{2,1,0:T(8,128)(2,1)}, u32[]{:S(2)}) copy-start(bf16[2,256,256]{2,1,0:T(8,128)(2,1)} %param.12) | copy-start | bytes 786436
  7.2 52.2 %all-gather.2.cloned.1.call-start = ((), (), s32[]{:S(2)}) async-start(), calls=%async_computation.5 | async-start | bytes 2088960 | tf_op jit(solution)/shard_map/all_gather | solution.py:47
  61.3 2.6 %copy-start.5 = (bf16[96,512]{1,0:T(8,128)(2,1)S(1)}, bf16[96,512]{1,0:T(8,128)(2,1)}, u32[]{:S(2)}) copy-start(bf16[96,512]{1,0:T(8,128)(2,1)} %param.17) | copy-start | bytes 294916
  66.7 11.7 %copy-start.4 = (s32[64]{0:T(128)S(1)}, s32[64]{0:T(128)}, u32[]{:S(2)}) copy-start(s32[64]{0:T(128)} %param.16) | copy-start | bytes 772
  69.1 19.4 %all-to-all-start = ((bf16[32,2,2176]{2,1,0:T(2,128)(2,1)}), bf16[32,2,2176]{2,1,0:T(2,128)(2,1)S(1)}, u32[]{:S(2)}, u32[]{:S(2)}) async-start(bf16[32,2,2176]{2,1,0:T(2,128)(2,1)} %reshape.228), calls=%async_computation | async-start | bytes 557056 | tf_op jit(solution)/shard_map/all_to_all | solution.py:11
  78.4 11.2 %copy-start.2 = (bf16[8,64,64]{2,1,0:T(8,128)(2,1)S(1)}, bf16[8,64,64]{2,1,0:T(8,128)(2,1)}, u32[]{:S(2)}) copy-start(bf16[8,64,64]{2,1,0:T(8,128)(2,1)} %param.13) | copy-start | bytes 196612
  89.4 1.5 copy-start.3
  92.8 16.7 %all-to-all-start.1 = ((bf16[32,2,2432]{2,1,0:T(2,128)(2,1)}), bf16[32,2,2432]{2,1,0:T(2,128)(2,1)S(1)}, u32[]{:S(2)}, u32[]{:S(2)}) async-start(bf16[32,2,2432]{2,1,0:T(2,128)(2,1)} %reshape.230), calls=%async_computation.1 | async-start | bytes 622592 | tf_op jit(solution)/shard_map/all_to_all | solution.py:11
  115.3 25.5 %all-to-all-start.2 = ((bf16[32,6,1536]{2,1,0:T(8,128)(2,1)}), bf16[32,6,1536]{2,1,0:T(8,128)(2,1)S(1)}, u32[]{:S(2)}, u32[]{:S(2)}) async-start(bf16[32,6,1536]{2,1,0:T(8,128)(2,1)} %convert_element_type.128), calls=%async_computation.2 | async-start | bytes 1572864 | tf_op jit(solution)/shard_map/all_to_all | solution.py:11
  122.1 63.3 %reduce-scatter.2.cloned.1.call-start = ((), (), s32[]{:S(2)}) async-start(), calls=%async_computation.6 | async-start | bytes 1253376 | tf_op jit(solution)/shard_map/reduce_scatter | solution.py:188
  142.3 47.5 %all-to-all-start.3 = ((f32[32,6,1536]{2,1,0:T(8,128)}), f32[32,6,1536]{2,1,0:T(8,128)S(1)}, u32[]{:S(2)}, u32[]{:S(2)}) async-start(f32[32,6,1536]{2,1,0:T(8,128)} %broadcast_in_dim.9), calls=%async_computation.3 | async-start | bytes 3145728 | tf_op jit(solution)/shard_map/all_to_all | solution.py:11
Sparse Core Ops, SparseCore 0:
  10.7 48.6 all-gather.1
  125.7 59.5 reduce-scatter.1

commit v8 on v7

--- a/solution.py
+++ b/solution.py
@@ -193,8 +193,9 @@
     d_second = fac_red[n_f : n_f + n_s].reshape(k_here, m_part, n_blk2)
     g_full = fac_red[n_f + n_s :].reshape(n_doc, lat)
 
-    gath5 = seq_exchange(jnp.broadcast_to(proj_red[None], (n_seq, rows_here, width)))
-    d_proj = gath5.reshape(2 * chan_rows, width)
+    proj_bf = proj_red.astype(jnp.bfloat16)
+    gath5 = seq_exchange(jnp.broadcast_to(proj_bf[None], (n_seq, rows_here, width)))
+    d_proj = gath5.reshape(2 * chan_rows, width).astype(jnp.float32)
     d_pooled = g_full * len_scale[:, None]
     d_down = jnp.einsum(
         "cd,dl->cl", xdoc, d_pooled.astype(jnp.bfloat16).astype(jnp.float32), precision=HIGHEST

time: 201 us -> 196 us (0.975)
  matrix products: 14.5 us -> 11.7 us
    reduce_scatter x1, waiting for transfers between devices: 33.4 us -> 14.4 us  [body(): lax.psum_scatter(fac_send.reshape(-1, 128), 'chan', scatter_dimension=0,...]
    all_to_all x4, waiting for transfers between devices: 36.4 us -> 53.9 us  [seq_exchange(): return lax.all_to_all(x, 'seq', 0, 0, tiled=True)]
  transfers between devices with their start and end apart: 6 -> 6, of which waited for: 5 -> 6; matrix products, arithmetic and copies ran while one was open for 6% -> 5% of each run, Pallas kernels for 0% -> 0%
where the time goes in v8:
time: 196 us; the launch traced here: 194 us
  waiting for transfers between devices  116 us (59%)
  starting transfers between devices  31.2 us (16%)
  local copies, waits for them, and re-layouts  15.4 us (8%)
  between operations  14.6 us (7%)
  matrix products  11.7 us (6%)
  other arithmetic  5.1 us (3%)
    all_to_all x4, waiting for transfers between devices, seq_exchange(): return lax.all_to_all(x, 'seq', 0, 0, tiled=True)  53.9 us
    all_gather x1, waiting for transfers between devices, body(): gathered_all = lax.all_gather(packed, 'chan', axis=0, tiled=True)  47.6 us
    all_to_all x4, starting transfers between devices, seq_exchange(): return lax.all_to_all(x, 'seq', 0, 0, tiled=True)  31.1 us
    reduce_scatter x1, waiting for transfers between devices, body(): lax.psum_scatter(fac_send.reshape(-1, 128), 'chan', scatter_dimension=0,...  14.4 us
  transfers between devices with their start and end apart: 6, of which 6 were waited for; matrix products, arithmetic and copies ran while one was open for 5% of the time, Pallas kernels for 0%

profile of v8, /device:TPU:1, one launch (start us, length us, event | category | flops | bytes accessed | tf_op | source)
XLA Modules:
  0.0 193.9 jit_solution(10338718657030272323)
XLA Ops:
  7.2 1.6 pad_maximum_fusion.2
  8.9 0.7 copy.85
  9.9 0.7 sub.12
  10.5 1.1 fusion.27
  11.8 47.6 %all-gather.2.cloned.1.call-done = bf16[1536,640]{1,0:T(8,128)(2,1)} async-done(((bf16[96,640]{1,0:T(8,128)(2,1)}), bf16[1536,640]{1,0:T(8,128)(2,1)}) %all-gather.2.cloned.1.call-update) | async-done | bytes 1966096 | tf_op jit(solution)/shard_map/all_gather | solution.py:47
  59.4 2.0 %convolution_convert_fusion.3 = bf16[512,96]{0,1:T(8,128)(2,1)S(1)} fusion(bf16[96,1536]{1,0:T(8,128)(2,1)} %param.11, bf16[1536,640]{1,0:T(8,128)(2,1)} %all-gather.2.cloned.1.call-done), kind=kOutput, calls=%fused_computation.6 | convolution fusion | flops 151044096 | bytes 1966080 | tf_op jit(solution)/shard_map/dot_general | solution.py:60
  61.4 0.2 fusion
  61.8 0.4 fusion.3
  62.2 0.3 fusion.35
  62.5 0.4 fusion.16
  63.3 0.3 reshape.193
  63.5 0.3 fusion.15
  64.2 0.5 broadcast.29
  64.7 0.8 reduce.2
  65.5 0.8 reshape.229
  66.3 9.3 %all-to-all-start = ((bf16[32,2,2176]{2,1,0:T(2,128)(2,1)}), bf16[32,2,2176]{2,1,0:T(2,128)(2,1)S(1)}, u32[]{:S(2)}, u32[]{:S(2)}) async-start(bf16[32,2,2176]{2,1,0:T(2,128)(2,1)} %reshape.229), calls=%async_computation | async-start | bytes 557056 | tf_op jit(solution)/shard_map/all_to_all | solution.py:11
  75.6 10.0 %all-to-all-done = bf16[32,2,2176]{2,1,0:T(2,128)(2,1)S(1)} async-done(((bf16[32,2,2176]{2,1,0:T(2,128)(2,1)}), bf16[32,2,2176]{2,1,0:T(2,128)(2,1)S(1)}, u32[]{:S(2)}, u32[]{:S(2)}) %all-to-all-start) | async-done | bytes 278560 | tf_op jit(solution)/shard_map/all_to_all | solution.py:11
  85.7 0.2 reshape.230
  86.2 0.3 reshape.201
  87.2 0.2 convolution_convert_fusion.2
  87.8 0.2 reshape.206
  88.4 0.8 reduce.3
  89.2 0.8 reshape.231
  90.0 6.8 %all-to-all-start.1 = ((bf16[32,2,2432]{2,1,0:T(2,128)(2,1)}), bf16[32,2,2432]{2,1,0:T(2,128)(2,1)S(1)}, u32[]{:S(2)}, u32[]{:S(2)}) async-start(bf16[32,2,2432]{2,1,0:T(2,128)(2,1)} %reshape.231), calls=%async_computation.1 | async-start | bytes 622592 | tf_op jit(solution)/shard_map/all_to_all | solution.py:11
  97.0 0.2 reshape.217
  97.3 9.4 %all-to-all-done.1 = bf16[32,2,2432]{2,1,0:T(2,128)(2,1)S(1)} async-done(((bf16[32,2,2432]{2,1,0:T(2,128)(2,1)}), bf16[32,2,2432]{2,1,0:T(2,128)(2,1)S(1)}, u32[]{:S(2)}, u32[]{:S(2)}) %all-to-all-start.1) | async-done | bytes 311328 | tf_op jit(solution)/shard_map/all_to_all | solution.py:11
  106.7 0.3 reshape.232
  107.0 0.3 reshape.210
  107.4 0.2 fusion.1
  108.3 1.0 fusion.10
  109.3 2.1 %convolution_convert_fusion = bf16[192,1536]{1,0:T(8,128)(2,1)S(1)} fusion(bf16[1536,640]{1,0:T(8,128)(2,1)} %all-gather.2.cloned.1.call-done, bf16[96,512]{1,0:T(8,128)(2,1)S(1)} %bitcast.139, bf16[96,512]{1,0:T(8,128)(2,1)S(1)} %get-tuple-element.9), kind=kOutput, calls=%fused_computation | convolution fusion | flops 302678016 | bytes 2359296 | tf_op jit(solution)/shard_map/ot,it->oi/dot_general | solution.py:170
  111.4 1.1 convert_element_type.131
  112.5 6.8 %all-to-all-start.2 = ((bf16[32,6,1536]{2,1,0:T(8,128)(2,1)}), bf16[32,6,1536]{2,1,0:T(8,128)(2,1)S(1)}, u32[]{:S(2)}, u32[]{:S(2)}) async-start(bf16[32,6,1536]{2,1,0:T(8,128)(2,1)} %convert_element_type.131), calls=%async_computation.2 | async-start | bytes 1572864 | tf_op jit(solution)/shard_map/all_to_all | solution.py:11
  119.4 0.3 copy.117
  119.9 1.2 reshape.218
  121.1 17.0 %all-to-all-done.2 = bf16[32,6,1536]{2,1,0:T(8,128)(2,1)S(1)} async-done(((bf16[32,6,1536]{2,1,0:T(8,128)(2,1)}), bf16[32,6,1536]{2,1,0:T(8,128)(2,1)S(1)}, u32[]{:S(2)}, u32[]{:S(2)}) %all-to-all-start.2) | async-done | bytes 589856 | tf_op jit(solution)/shard_map/all_to_all | solution.py:11
  138.2 1.0 broadcast_in_dim.9
  139.2 8.3 %all-to-all-start.3 = ((bf16[32,6,1536]{2,1,0:T(8,128)(2,1)}), bf16[32,6,1536]{2,1,0:T(8,128)(2,1)S(1)}, u32[]{:S(2)}, u32[]{:S(2)}) async-start(bf16[32,6,1536]{2,1,0:T(8,128)(2,1)} %broadcast_in_dim.9), calls=%async_computation.3 | async-start | bytes 1572864 | tf_op jit(solution)/shard_map/all_to_all | solution.py:11
  147.9 0.9 fusion.42
  148.8 17.5 %all-to-all-done.3 = bf16[32,6,1536]{2,1,0:T(8,128)(2,1)S(1)} async-done(((bf16[32,6,1536]{2,1,0:T(8,128)(2,1)}), bf16[32,6,1536]{2,1,0:T(8,128)(2,1)S(1)}, u32[]{:S(2)}, u32[]{:S(2)}) %all-to-all-start.3) | async-done | bytes 589856 | tf_op jit(solution)/shard_map/all_to_all | solution.py:11
  166.5 0.9 slice.126
  167.4 0.9 slice.124
  168.3 14.4 %reduce-scatter.2.cloned.1.call-done = f32[144,128]{1,0:T(8,128)} async-done(((f32[2304,128]{1,0:T(8,128)}), f32[144,128]{1,0:T(8,128)}) %reduce-scatter.2.cloned.1.call-update) | async-done | bytes 73744 | tf_op jit(solution)/shard_map/reduce_scatter | solution.py:188
  182.7 0.7 slice.150
  183.4 0.7 reshape.220
  184.1 0.8 slice.149
  184.8 0.6 reshape.219
  185.5 1.6 fusion.29
  (76 shorter events, 4.8 us)
Async XLA Ops:
  7.2 55.3 %copy-start = (bf16[96,1536]{1,0:T(8,128)(2,1)S(1)}, bf16[96,1536]{1,0:T(8,128)(2,1)}, u32[]{:S(2)}) copy-start(bf16[96,1536]{1,0:T(8,128)(2,1)} %param.10) | copy-start | bytes 884740
  7.2 54.2 %copy-start.1 = (bf16[2,256,256]{2,1,0:T(8,128)(2,1)S(1)}, bf16[2,256,256]{2,1,0:T(8,128)(2,1)}, u32[]{:S(2)}) copy-start(bf16[2,256,256]{2,1,0:T(8,128)(2,1)} %param.12) | copy-start | bytes 786436
  7.2 52.2 %all-gather.2.cloned.1.call-start = ((), (), s32[]{:S(2)}) async-start(), calls=%async_computation.5 | async-start | bytes 2088960 | tf_op jit(solution)/shard_map/all_gather | solution.py:47
  59.4 2.4 %copy-start.5 = (bf16[1536,640]{1,0:T(8,128)(2,1)S(1)}, bf16[1536,640]{1,0:T(8,128)(2,1)}, u32[]{:S(2)}) copy-start(bf16[1536,640]{1,0:T(8,128)(2,1)} %all-gather.2.cloned.1.call-done) | copy-start | bytes 5898244
  61.4 1.1 copy-start.6
  63.8 11.7 %copy-start.4 = (s32[64]{0:T(128)S(1)}, s32[64]{0:T(128)}, u32[]{:S(2)}) copy-start(s32[64]{0:T(128)} %param.16) | copy-start | bytes 772
  66.3 19.4 %all-to-all-start = ((bf16[32,2,2176]{2,1,0:T(2,128)(2,1)}), bf16[32,2,2176]{2,1,0:T(2,128)(2,1)S(1)}, u32[]{:S(2)}, u32[]{:S(2)}) async-start(bf16[32,2,2176]{2,1,0:T(2,128)(2,1)} %reshape.229), calls=%async_computation | async-start | bytes 557056 | tf_op jit(solution)/shard_map/all_to_all | solution.py:11
  75.6 11.2 %copy-start.2 = (bf16[8,64,64]{2,1,0:T(8,128)(2,1)S(1)}, bf16[8,64,64]{2,1,0:T(8,128)(2,1)}, u32[]{:S(2)}) copy-start(bf16[8,64,64]{2,1,0:T(8,128)(2,1)} %param.13) | copy-start | bytes 196612
  86.6 1.5 copy-start.3
  90.0 16.7 %all-to-all-start.1 = ((bf16[32,2,2432]{2,1,0:T(2,128)(2,1)}), bf16[32,2,2432]{2,1,0:T(2,128)(2,1)S(1)}, u32[]{:S(2)}, u32[]{:S(2)}) async-start(bf16[32,2,2432]{2,1,0:T(2,128)(2,1)} %reshape.231), calls=%async_computation.1 | async-start | bytes 622592 | tf_op jit(solution)/shard_map/all_to_all | solution.py:11
  112.5 25.6 %all-to-all-start.2 = ((bf16[32,6,1536]{2,1,0:T(8,128)(2,1)}), bf16[32,6,1536]{2,1,0:T(8,128)(2,1)S(1)}, u32[]{:S(2)}, u32[]{:S(2)}) async-start(bf16[32,6,1536]{2,1,0:T(8,128)(2,1)} %convert_element_type.131), calls=%async_computation.2 | async-start | bytes 1572864 | tf_op jit(solution)/shard_map/all_to_all | solution.py:11
  119.3 63.4 %reduce-scatter.2.cloned.1.call-start = ((), (), s32[]{:S(2)}) async-start(), calls=%async_computation.6 | async-start | bytes 1253376 | tf_op jit(solution)/shard_map/reduce_scatter | solution.py:188
  139.2 27.1 %all-to-all-start.3 = ((bf16[32,6,1536]{2,1,0:T(8,128)(2,1)}), bf16[32,6,1536]{2,1,0:T(8,128)(2,1)S(1)}, u32[]{:S(2)}, u32[]{:S(2)}) async-start(bf16[32,6,1536]{2,1,0:T(8,128)(2,1)} %broadcast_in_dim.9), calls=%async_computation.3 | async-start | bytes 1572864 | tf_op jit(solution)/shard_map/all_to_all | solution.py:11
Sparse Core Ops, SparseCore 0:
  10.7 48.6 all-gather.1
  123.0 59.6 reduce-scatter.1

commit v9 on v8

--- a/solution.py
+++ b/solution.py
@@ -186,20 +186,17 @@
     g_send = jnp.broadcast_to(g_gath, (n_chan, n_doc * lat))
     fac_send = jnp.concatenate([first_send, second_send, g_send], axis=1)
     fac_red = lax.psum_scatter(fac_send.reshape(-1, 128), "chan", scatter_dimension=0, tiled=True)
+    proj_bf = proj_red.astype(jnp.bfloat16)
+    gath5 = seq_exchange(jnp.broadcast_to(proj_bf[None], (n_seq, rows_here, width)))
     fac_red = fac_red.reshape(-1)
     n_f = blocks_here * k_part * block_width
     d_first = fac_red[:n_f].reshape(blocks_here, k_part, block_width)
     n_s = k_here * m_part * n_blk2
     d_second = fac_red[n_f : n_f + n_s].reshape(k_here, m_part, n_blk2)
     g_full = fac_red[n_f + n_s :].reshape(n_doc, lat)
-
-    proj_bf = proj_red.astype(jnp.bfloat16)
-    gath5 = seq_exchange(jnp.broadcast_to(proj_bf[None], (n_seq, rows_here, width)))
+    d_pooled = lax.reduce_precision(g_full * len_scale[:, None], exponent_bits=8, mantissa_bits=7)
+    d_down = jnp.einsum("cd,dl->cl", xdoc, d_pooled, precision=HIGHEST)
     d_proj = gath5.reshape(2 * chan_rows, width).astype(jnp.float32)
-    d_pooled = g_full * len_scale[:, None]
-    d_down = jnp.einsum(
-        "cd,dl->cl", xdoc, d_pooled.astype(jnp.bfloat16).astype(jnp.float32), precision=HIGHEST
-    )
     return (hidden, d_proj[:chan_rows], d_proj[chan_rows:], d_first, d_second, d_down, d_up)
 
 

time: 196 us -> 196 us (level)
  no operation moved by 1% of the time
where the time goes in v9:
time: 196 us; the launch traced here: 194 us
  waiting for transfers between devices  116 us (59%)
  starting transfers between devices  31.2 us (16%)
  local copies, waits for them, and re-layouts  15.4 us (8%)
  between operations  14.6 us (7%)
  matrix products  11.8 us (6%)
  other arithmetic  5.1 us (3%)
    all_to_all x4, waiting for transfers between devices, seq_exchange(): return lax.all_to_all(x, 'seq', 0, 0, tiled=True)  53.9 us
    all_gather x1, waiting for transfers between devices, body(): gathered_all = lax.all_gather(packed, 'chan', axis=0, tiled=True)  47.6 us
    all_to_all x4, starting transfers between devices, seq_exchange(): return lax.all_to_all(x, 'seq', 0, 0, tiled=True)  31.1 us
    reduce_scatter x1, waiting for transfers between devices, body(): lax.psum_scatter(fac_send.reshape(-1, 128), 'chan', scatter_dimension=0,...  14.4 us
  transfers between devices with their start and end apart: 6, of which 6 were waited for; matrix products, arithmetic and copies ran while one was open for 5% of the time, Pallas kernels for 0%

profile of v9, /device:TPU:1, one launch (start us, length us, event | category | flops | bytes accessed | tf_op | source)
XLA Modules:
  0.0 194.0 jit_solution(387574804326421877)
XLA Ops:
  7.2 1.6 pad_maximum_fusion.2
  8.9 0.7 copy.85
  9.9 0.7 sub.12
  10.5 1.1 fusion.27
  11.8 47.6 %all-gather.2.cloned.1.call-done = bf16[1536,640]{1,0:T(8,128)(2,1)} async-done(((bf16[96,640]{1,0:T(8,128)(2,1)}), bf16[1536,640]{1,0:T(8,128)(2,1)}) %all-gather.2.cloned.1.call-update) | async-done | bytes 1966096 | tf_op jit(solution)/shard_map/all_gather | solution.py:47
  59.4 2.0 %convolution_convert_fusion.3 = bf16[512,96]{0,1:T(8,128)(2,1)S(1)} fusion(bf16[96,1536]{1,0:T(8,128)(2,1)} %param.11, bf16[1536,640]{1,0:T(8,128)(2,1)} %all-gather.2.cloned.1.call-done), kind=kOutput, calls=%fused_computation.6 | convolution fusion | flops 151044096 | bytes 1966080 | tf_op jit(solution)/shard_map/dot_general | solution.py:60
  61.4 0.2 fusion
  61.8 0.4 fusion.3
  62.2 0.3 fusion.35
  62.5 0.4 fusion.16
  63.3 0.3 reshape.193
  63.5 0.3 fusion.15
  64.2 0.5 broadcast.29
  64.7 0.8 reduce.2
  65.5 0.8 reshape.229
  66.3 9.3 %all-to-all-start = ((bf16[32,2,2176]{2,1,0:T(2,128)(2,1)}), bf16[32,2,2176]{2,1,0:T(2,128)(2,1)S(1)}, u32[]{:S(2)}, u32[]{:S(2)}) async-start(bf16[32,2,2176]{2,1,0:T(2,128)(2,1)} %reshape.229), calls=%async_computation | async-start | bytes 557056 | tf_op jit(solution)/shard_map/all_to_all | solution.py:11
  75.6 10.0 %all-to-all-done = bf16[32,2,2176]{2,1,0:T(2,128)(2,1)S(1)} async-done(((bf16[32,2,2176]{2,1,0:T(2,128)(2,1)}), bf16[32,2,2176]{2,1,0:T(2,128)(2,1)S(1)}, u32[]{:S(2)}, u32[]{:S(2)}) %all-to-all-start) | async-done | bytes 278560 | tf_op jit(solution)/shard_map/all_to_all | solution.py:11
  85.7 0.2 reshape.230
  86.2 0.3 reshape.201
  87.2 0.2 convolution_convert_fusion.2
  87.8 0.2 reshape.206
  88.4 0.8 reduce.3
  89.2 0.8 reshape.231
  90.0 6.8 %all-to-all-start.1 = ((bf16[32,2,2432]{2,1,0:T(2,128)(2,1)}), bf16[32,2,2432]{2,1,0:T(2,128)(2,1)S(1)}, u32[]{:S(2)}, u32[]{:S(2)}) async-start(bf16[32,2,2432]{2,1,0:T(2,128)(2,1)} %reshape.231), calls=%async_computation.1 | async-start | bytes 622592 | tf_op jit(solution)/shard_map/all_to_all | solution.py:11
  97.0 0.2 reshape.217
  97.3 9.4 %all-to-all-done.1 = bf16[32,2,2432]{2,1,0:T(2,128)(2,1)S(1)} async-done(((bf16[32,2,2432]{2,1,0:T(2,128)(2,1)}), bf16[32,2,2432]{2,1,0:T(2,128)(2,1)S(1)}, u32[]{:S(2)}, u32[]{:S(2)}) %all-to-all-start.1) | async-done | bytes 311328 | tf_op jit(solution)/shard_map/all_to_all | solution.py:11
  106.7 0.3 reshape.232
  107.0 0.3 reshape.210
  107.4 0.2 fusion.1
  108.3 1.0 fusion.10
  109.3 2.1 %convolution_convert_fusion = bf16[192,1536]{1,0:T(8,128)(2,1)S(1)} fusion(bf16[1536,640]{1,0:T(8,128)(2,1)} %all-gather.2.cloned.1.call-done, bf16[96,512]{1,0:T(8,128)(2,1)S(1)} %bitcast.139, bf16[96,512]{1,0:T(8,128)(2,1)S(1)} %get-tuple-element.9), kind=kOutput, calls=%fused_computation | convolution fusion | flops 302678016 | bytes 2359296 | tf_op jit(solution)/shard_map/ot,it->oi/dot_general | solution.py:170
  111.4 1.1 convert_element_type.126
  112.5 6.8 %all-to-all-start.2 = ((bf16[32,6,1536]{2,1,0:T(8,128)(2,1)}), bf16[32,6,1536]{2,1,0:T(8,128)(2,1)S(1)}, u32[]{:S(2)}, u32[]{:S(2)}) async-start(bf16[32,6,1536]{2,1,0:T(8,128)(2,1)} %convert_element_type.126), calls=%async_computation.2 | async-start | bytes 1572864 | tf_op jit(solution)/shard_map/all_to_all | solution.py:11
  119.4 0.3 copy.117
  119.9 1.2 reshape.218
  121.1 17.0 %all-to-all-done.2 = bf16[32,6,1536]{2,1,0:T(8,128)(2,1)S(1)} async-done(((bf16[32,6,1536]{2,1,0:T(8,128)(2,1)}), bf16[32,6,1536]{2,1,0:T(8,128)(2,1)S(1)}, u32[]{:S(2)}, u32[]{:S(2)}) %all-to-all-start.2) | async-done | bytes 589856 | tf_op jit(solution)/shard_map/all_to_all | solution.py:11
  138.2 1.0 broadcast_in_dim.9
  139.2 8.3 %all-to-all-start.3 = ((bf16[32,6,1536]{2,1,0:T(8,128)(2,1)}), bf16[32,6,1536]{2,1,0:T(8,128)(2,1)S(1)}, u32[]{:S(2)}, u32[]{:S(2)}) async-start(bf16[32,6,1536]{2,1,0:T(8,128)(2,1)} %broadcast_in_dim.9), calls=%async_computation.3 | async-start | bytes 1572864 | tf_op jit(solution)/shard_map/all_to_all | solution.py:11
  147.9 0.9 fusion.42
  148.8 17.5 %all-to-all-done.3 = bf16[32,6,1536]{2,1,0:T(8,128)(2,1)S(1)} async-done(((bf16[32,6,1536]{2,1,0:T(8,128)(2,1)}), bf16[32,6,1536]{2,1,0:T(8,128)(2,1)S(1)}, u32[]{:S(2)}, u32[]{:S(2)}) %all-to-all-start.3) | async-done | bytes 589856 | tf_op jit(solution)/shard_map/all_to_all | solution.py:11
  166.5 0.9 slice.126
  167.4 0.9 slice.124
  168.3 14.4 %reduce-scatter.2.cloned.1.call-done = f32[144,128]{1,0:T(8,128)} async-done(((f32[2304,128]{1,0:T(8,128)}), f32[144,128]{1,0:T(8,128)}) %reduce-scatter.2.cloned.1.call-update) | async-done | bytes 73744 | tf_op jit(solution)/shard_map/reduce_scatter | solution.py:188
  182.7 0.7 slice.150
  183.4 0.7 reshape.220
  184.1 0.8 slice.149
  184.8 0.6 reshape.219
  185.5 1.7 fusion.29
  (76 shorter events, 4.8 us)
Async XLA Ops:
  7.2 55.3 %copy-start = (bf16[96,1536]{1,0:T(8,128)(2,1)S(1)}, bf16[96,1536]{1,0:T(8,128)(2,1)}, u32[]{:S(2)}) copy-start(bf16[96,1536]{1,0:T(8,128)(2,1)} %param.10) | copy-start | bytes 884740
  7.2 54.2 %copy-start.1 = (bf16[2,256,256]{2,1,0:T(8,128)(2,1)S(1)}, bf16[2,256,256]{2,1,0:T(8,128)(2,1)}, u32[]{:S(2)}) copy-start(bf16[2,256,256]{2,1,0:T(8,128)(2,1)} %param.12) | copy-start | bytes 786436
  7.2 52.2 %all-gather.2.cloned.1.call-start = ((), (), s32[]{:S(2)}) async-start(), calls=%async_computation.5 | async-start | bytes 2088960 | tf_op jit(solution)/shard_map/all_gather | solution.py:47
  59.4 2.4 %copy-start.5 = (bf16[1536,640]{1,0:T(8,128)(2,1)S(1)}, bf16[1536,640]{1,0:T(8,128)(2,1)}, u32[]{:S(2)}) copy-start(bf16[1536,640]{1,0:T(8,128)(2,1)} %all-gather.2.cloned.1.call-done) | copy-start | bytes 5898244
  61.4 1.1 copy-start.6
  63.8 11.7 %copy-start.4 = (s32[64]{0:T(128)S(1)}, s32[64]{0:T(128)}, u32[]{:S(2)}) copy-start(s32[64]{0:T(128)} %param.16) | copy-start | bytes 772
  66.3 19.4 %all-to-all-start = ((bf16[32,2,2176]{2,1,0:T(2,128)(2,1)}), bf16[32,2,2176]{2,1,0:T(2,128)(2,1)S(1)}, u32[]{:S(2)}, u32[]{:S(2)}) async-start(bf16[32,2,2176]{2,1,0:T(2,128)(2,1)} %reshape.229), calls=%async_computation | async-start | bytes 557056 | tf_op jit(solution)/shard_map/all_to_all | solution.py:11
  75.6 11.2 %copy-start.2 = (bf16[8,64,64]{2,1,0:T(8,128)(2,1)S(1)}, bf16[8,64,64]{2,1,0:T(8,128)(2,1)}, u32[]{:S(2)}) copy-start(bf16[8,64,64]{2,1,0:T(8,128)(2,1)} %param.13) | copy-start | bytes 196612
  86.6 1.5 copy-start.3
  90.0 16.7 %all-to-all-start.1 = ((bf16[32,2,2432]{2,1,0:T(2,128)(2,1)}), bf16[32,2,2432]{2,1,0:T(2,128)(2,1)S(1)}, u32[]{:S(2)}, u32[]{:S(2)}) async-start(bf16[32,2,2432]{2,1,0:T(2,128)(2,1)} %reshape.231), calls=%async_computation.1 | async-start | bytes 622592 | tf_op jit(solution)/shard_map/all_to_all | solution.py:11
  112.5 25.6 %all-to-all-start.2 = ((bf16[32,6,1536]{2,1,0:T(8,128)(2,1)}), bf16[32,6,1536]{2,1,0:T(8,128)(2,1)S(1)}, u32[]{:S(2)}, u32[]{:S(2)}) async-start(bf16[32,6,1536]{2,1,0:T(8,128)(2,1)} %convert_element_type.126), calls=%async_computation.2 | async-start | bytes 1572864 | tf_op jit(solution)/shard_map/all_to_all | solution.py:11
  119.3 63.4 %reduce-scatter.2.cloned.1.call-start = ((), (), s32[]{:S(2)}) async-start(), calls=%async_computation.6 | async-start | bytes 1253376 | tf_op jit(solution)/shard_map/reduce_scatter | solution.py:188
  139.2 27.1 %all-to-all-start.3 = ((bf16[32,6,1536]{2,1,0:T(8,128)(2,1)}), bf16[32,6,1536]{2,1,0:T(8,128)(2,1)S(1)}, u32[]{:S(2)}, u32[]{:S(2)}) async-start(bf16[32,6,1536]{2,1,0:T(8,128)(2,1)} %broadcast_in_dim.9), calls=%async_computation.3 | async-start | bytes 1572864 | tf_op jit(solution)/shard_map/all_to_all | solution.py:11
Sparse Core Ops, SparseCore 0:
  10.7 48.6 all-gather.1
  123.0 59.6 reduce-scatter.1
